TPU v7x, 512 devices: a whole 4x8x8 slice. The times are simulated.
512 devices in a mesh: elem: 64 (over z, y), mode: 8 (over x, core).
Axes of the slice: x: 4, y: 8, z: 8, core: 2. Of those that a mesh axis runs over, the one named last changes fastest.
Arguments:
- levels_rhs: float32 [128, 262144], P(None, ('elem', 'mode')), may hold values from -6 to 6
- to_modes: float32 [128, 128], replicated, may hold values from -0.5 to 0.5
- from_modes: float32 [128, 128], replicated, may hold values from -0.5 to 0.5
- helmholtz: float32 [128], replicated, may hold values from 0.5 to 50
- local_inverse: float32 [16, 16], replicated
- neighbor_ids: int32 [8, 16384], P(None, 'elem'), may hold values from 0 to 511, as said below
- neighbor_count: int32 [16384], P('elem'), may hold values from 7 to 8
- orientation: int32 [8, 16384], P(None, 'elem'), may hold values from 0 to 7
Outputs:
- levels_out: float32 [128, 262144], P(None, ('elem', 'mode'))
Inputs may be any that keep to these rules, and one draw needn't show every extreme that they name: `neighbor_ids`: neighbour ids of an element of local index i in its elem block lie within i to i + 256.
All inputs are finite; a program needn't handle non-finite values.
Results may differ from a plain program's by a relative error of at most 0.0001.
Values sent between devices are 32-bit elements; how exact they have to be, the bound alone decides.
No kernel may reach another device: no remote copies, remote signals or barrier semaphores. Data moves between devices by JAX's collectives and lax.ppermute only.
A program may use at most 64 MiB of HBM per device.

v0:
```python
import jax
import jax.numpy as jnp
from jax import lax
from jax.sharding import PartitionSpec as P


def padded(block, sides, width):
    for axis, dim in sides:
        count = lax.axis_size(axis)
        forward = [(i, i + 1) for i in range(count - 1)]
        forward.append((count - 1, 0))
        backward = [(target, source) for source, target in forward]
        low = lax.ppermute(
            lax.slice_in_dim(block, block.shape[dim] - width, None, axis=dim), axis, forward
        )
        high = lax.ppermute(lax.slice_in_dim(block, 0, width, axis=dim), axis, backward)
        block = jnp.concatenate([low, block, high], axis=dim)
    return block


def oriented_points(code, points):
    row = points // 4
    col = points % 4
    swap = code % 2
    flip_row = code // 2 % 2
    flip_col = code // 4 % 2
    row_two = jnp.where(swap == 1, col, row)
    col_two = jnp.where(swap == 1, row, col)
    row_three = jnp.where(flip_row == 1, 3 - row_two, row_two)
    col_three = jnp.where(flip_col == 1, 3 - col_two, col_two)
    return row_three * 4 + col_three


def schwarz_sweep(u_own, u_ext, rhs_part, index, orientation, count, coeff, local_inverse):
    modes = u_ext.shape[0]
    width = u_ext.shape[2]
    elems = index.shape[1]
    flat = u_ext.reshape(modes, 16 * width)
    points = jnp.arange(16, dtype=jnp.int32)[:, None]
    total = jnp.zeros((modes, 16, elems), jnp.float32)
    for slot in range(8):
        perm = oriented_points(orientation[slot][None, :], points)
        where_at = perm * width + index[slot][None, :]
        picked = jnp.take(flat, where_at.reshape(-1), axis=1).reshape(modes, 16, elems)
        used = (slot < count)[None, None, :]
        total = total + jnp.where(used, picked, 0.0)
    scale = coeff[:, None, None]
    countf = count.astype(jnp.float32)[None, None, :]
    resid = rhs_part - (1.0 + scale) * u_own + scale * total / countf
    fix = jnp.einsum("pq,mqe->mpe", local_inverse, resid, precision=lax.Precision.HIGHEST)
    return u_own + fix / (1.0 + scale)


def body(
    levels_rhs,
    to_modes,
    from_modes,
    helmholtz,
    local_inverse,
    neighbor_ids,
    neighbor_count,
    orientation,
):
    groups = lax.axis_size("mode")
    group_modes = to_modes.shape[0] // groups
    first_mode = lax.axis_index("mode") * group_modes
    coeff = lax.dynamic_slice_in_dim(helmholtz, first_mode, group_modes, 0)
    all_modes = jnp.dot(to_modes, levels_rhs, precision=lax.Precision.HIGHEST)
    rhs_flat = lax.all_to_all(all_modes, "mode", split_axis=0, concat_axis=1, tiled=True)
    block = rhs_flat.shape[1] // 16
    rhs_modes = jnp.transpose(rhs_flat.reshape(group_modes, block, 16), (0, 2, 1))
    halo_width = block // 2
    u_start = rhs_modes / (1.0 + coeff[:, None, None])
    u_now = u_start
    for sweep_index in range(2):
        u_ext = padded(u_now, (("elem", 2),), halo_width)
        u_now = schwarz_sweep(
            u_now, u_ext, rhs_modes, neighbor_ids, orientation, neighbor_count, coeff, local_inverse
        )
    u_flat = jnp.transpose(u_now, (0, 2, 1)).reshape(group_modes, block * 16)
    all_levels = lax.all_to_all(u_flat, "mode", split_axis=1, concat_axis=0, tiled=True)
    return jnp.dot(from_modes, all_levels, precision=lax.Precision.HIGHEST)


def solution(mesh):
    in_specs = (
        P(None, ("elem", "mode")),
        P(),
        P(),
        P(),
        P(),
        P(None, "elem"),
        P("elem"),
        P(None, "elem"),
    )
    out_specs = P(None, ("elem", "mode"))
    return jax.shard_map(body, mesh=mesh, in_specs=in_specs, out_specs=out_specs, check_vma=False)
```

profile of v0, /device:TPU:1, one launch (start us, length us, event | category | flops | bytes accessed | tf_op | source)
XLA Modules:
  0.0 410.9 jit_solution(3906040305538114303)
XLA Ops:
  0.0 0.9 copy-done
  1.0 1.9 fusion.120
  2.9 10.2 %all-to-all-start = ((f32[8,16,512]{2,1,0:T(8,128)}), f32[8,16,512]{2,1,0:T(8,128)S(1)}, u32[]{:S(2)}, u32[]{:S(2)}) async-start(f32[8,16,512]{2,1,0:T(8,128)} %bitcast), calls=%async_computation | async-start | bytes 524288 | tf_op jit(solution)/shard_map/all_to_all | solution.py:69
  13.1 1.0 negate_select_fusion.8
  14.1 1.2 compare_reduce_fusion.23
  15.5 1.0 fusion.119
  21.4 0.7 reshape.239
  22.8 1.9 collective-permute-start
  24.8 9.4 %collective-permute-start.1 = (f32[16,16,128]{2,1,0:T(8,128)S(1)}, f32[16,16,128]{2,1,0:T(8,128)S(1)}, u32[]{:S(2)}, u32[]{:S(2)}) collective-permute-start(f32[16,16,128]{2,1,0:T(8,128)S(1)} %get-tuple-element.51), channel_id=1, source_target_pairs={{8,0},{16,8},{24,16},{32,24},{40,32},{48,40},{56,48},{64,56},{72,6... | collective-permute-start | bytes 393224 | tf_op jit(solution)/shard_map/ppermute | solution.py:16
  34.7 1.1 collective-permute-done
  35.9 1.0 collective-permute-done.1
  36.9 2.6 copy.134
  39.5 16.3 %gather_fusion = f32[4096,16]{1,0:T(8,128)} fusion(f32[16,8192]{0,1:T(8,128)} %bitcast.173, s32[4096]{0:T(1024)S(1)} %broadcast_clamp_fusion.7), kind=kCustom, calls=%fused_computation.clone | custom fusion | bytes 540672 | tf_op jit(solution)/shard_map/jit(_take)/gather | solution.py:44
  55.8 3.6 broadcast_select_fusion.15
  60.0 16.3 %gather_fusion.1 = f32[4096,16]{1,0:T(8,128)} fusion(f32[16,8192]{0,1:T(8,128)} %bitcast.174, s32[4096]{0:T(1024)S(1)} %broadcast_clamp_fusion.6), kind=kCustom, calls=%fused_computation.1.clone | custom fusion | bytes 540672 | tf_op jit(solution)/shard_map/jit(_take)/gather | solution.py:44
  76.3 3.6 broadcast_select_fusion.14
  80.5 16.3 %gather_fusion.2 = f32[4096,16]{1,0:T(8,128)} fusion(f32[16,8192]{0,1:T(8,128)} %bitcast.175, s32[4096]{0:T(1024)S(1)} %broadcast_clamp_fusion.5), kind=kCustom, calls=%fused_computation.2.clone | custom fusion | bytes 540672 | tf_op jit(solution)/shard_map/jit(_take)/gather | solution.py:44
  96.8 3.6 broadcast_select_fusion.13
  101.0 16.3 %gather_fusion.3 = f32[4096,16]{1,0:T(8,128)} fusion(f32[16,8192]{0,1:T(8,128)} %bitcast.176, s32[4096]{0:T(1024)S(1)} %broadcast_clamp_fusion.4), kind=kCustom, calls=%fused_computation.3.clone | custom fusion | bytes 540672 | tf_op jit(solution)/shard_map/jit(_take)/gather | solution.py:44
  117.3 3.6 broadcast_select_fusion.12
  120.9 1.3 copy.121
  122.2 16.3 %gather_fusion.4 = f32[4096,16]{1,0:T(8,128)} fusion(f32[16,8192]{0,1:T(8,128)} %bitcast.177, s32[4096]{0:T(1024)S(1)} %broadcast_clamp_fusion.3), kind=kCustom, calls=%fused_computation.4.clone | custom fusion | bytes 540672 | tf_op jit(solution)/shard_map/jit(_take)/gather | solution.py:44
  138.5 3.6 broadcast_select_fusion.11
  142.1 1.3 copy.122
  143.5 16.3 %gather_fusion.5 = f32[4096,16]{1,0:T(8,128)} fusion(f32[16,8192]{0,1:T(8,128)} %bitcast.178, s32[4096]{0:T(1024)S(1)} %broadcast_clamp_fusion.2), kind=kCustom, calls=%fused_computation.5.clone | custom fusion | bytes 540672 | tf_op jit(solution)/shard_map/jit(_take)/gather | solution.py:44
  159.7 3.6 broadcast_select_fusion.10
  163.4 1.3 copy.123
  164.7 16.3 %gather_fusion.6 = f32[4096,16]{1,0:T(8,128)} fusion(f32[16,8192]{0,1:T(8,128)} %bitcast.179, s32[4096]{0:T(1024)S(1)} %broadcast_clamp_fusion.1), kind=kCustom, calls=%fused_computation.6.clone | custom fusion | bytes 540672 | tf_op jit(solution)/shard_map/jit(_take)/gather | solution.py:44
  181.0 3.6 broadcast_select_fusion.9
  184.6 1.3 copy.124
  185.9 16.3 %gather_fusion.7 = f32[4096,16]{1,0:T(8,128)} fusion(f32[16,8192]{0,1:T(8,128)} %bitcast.180, s32[4096]{0:T(1024)S(1)} %broadcast_clamp_fusion), kind=kCustom, calls=%fused_computation.7.clone | custom fusion | bytes 540672 | tf_op jit(solution)/shard_map/jit(_take)/gather | solution.py:44
  202.2 3.6 broadcast_select_fusion.8
  205.8 1.3 copy.125
  207.1 2.6 bitcast_add_fusion
  209.7 1.9 collective-permute-start.2
  211.6 7.7 %collective-permute-start.3 = (f32[16,16,128]{2,1,0:T(8,128)S(1)}, f32[16,16,128]{2,1,0:T(8,128)S(1)}, u32[]{:S(2)}, u32[]{:S(2)}) collective-permute-start(f32[16,16,128]{2,1,0:T(8,128)S(1)} %get-tuple-element.49), channel_id=1, source_target_pairs={{8,0},{16,8},{24,16},{32,24},{40,32},{48,40},{56,48},{64,56},{72,6... | collective-permute-start | bytes 393224 | tf_op jit(solution)/shard_map/ppermute | solution.py:16
  219.3 0.9 collective-permute-done.2
  220.2 0.8 collective-permute-done.3
  221.1 2.6 copy.135
  223.7 16.3 %gather_fusion.8 = f32[4096,16]{1,0:T(8,128)} fusion(f32[16,8192]{0,1:T(8,128)} %bitcast.181, s32[4096]{0:T(1024)S(1)} %broadcast_clamp_fusion.7), kind=kCustom, calls=%fused_computation.8.clone | custom fusion | bytes 540672 | tf_op jit(solution)/shard_map/jit(_take)/gather | solution.py:44
  239.9 16.3 %gather_fusion.9 = f32[4096,16]{1,0:T(8,128)} fusion(f32[16,8192]{0,1:T(8,128)} %bitcast.182, s32[4096]{0:T(1024)S(1)} %broadcast_clamp_fusion.6), kind=kCustom, calls=%fused_computation.9.clone | custom fusion | bytes 540672 | tf_op jit(solution)/shard_map/jit(_take)/gather | solution.py:44
  256.2 16.3 %gather_fusion.10 = f32[4096,16]{1,0:T(8,128)} fusion(f32[16,8192]{0,1:T(8,128)} %bitcast.183, s32[4096]{0:T(1024)S(1)} %broadcast_clamp_fusion.5), kind=kCustom, calls=%fused_computation.10.clone | custom fusion | bytes 540672 | tf_op jit(solution)/shard_map/jit(_take)/gather | solution.py:44
  272.4 16.3 %gather_fusion.11 = f32[4096,16]{1,0:T(8,128)} fusion(f32[16,8192]{0,1:T(8,128)} %bitcast.184, s32[4096]{0:T(1024)S(1)} %broadcast_clamp_fusion.4), kind=kCustom, calls=%fused_computation.11.clone | custom fusion | bytes 540672 | tf_op jit(solution)/shard_map/jit(_take)/gather | solution.py:44
  288.7 16.3 %gather_fusion.12 = f32[4096,16]{1,0:T(8,128)} fusion(f32[16,8192]{0,1:T(8,128)} %bitcast.185, s32[4096]{0:T(1024)S(1)} %broadcast_clamp_fusion.3), kind=kCustom, calls=%fused_computation.12.clone | custom fusion | bytes 540672 | tf_op jit(solution)/shard_map/jit(_take)/gather | solution.py:44
  305.0 16.3 %gather_fusion.13 = f32[4096,16]{1,0:T(8,128)} fusion(f32[16,8192]{0,1:T(8,128)} %bitcast.186, s32[4096]{0:T(1024)S(1)} %broadcast_clamp_fusion.2), kind=kCustom, calls=%fused_computation.13.clone | custom fusion | bytes 540672 | tf_op jit(solution)/shard_map/jit(_take)/gather | solution.py:44
  321.2 16.3 %gather_fusion.14 = f32[4096,16]{1,0:T(8,128)} fusion(f32[16,8192]{0,1:T(8,128)} %bitcast.187, s32[4096]{0:T(1024)S(1)} %broadcast_clamp_fusion.1), kind=kCustom, calls=%fused_computation.14.clone | custom fusion | bytes 540672 | tf_op jit(solution)/shard_map/jit(_take)/gather | solution.py:44
  337.5 16.3 %gather_fusion.15 = f32[4096,16]{1,0:T(8,128)} fusion(f32[16,8192]{0,1:T(8,128)} %bitcast.188, s32[4096]{0:T(1024)S(1)} %broadcast_clamp_fusion), kind=kCustom, calls=%fused_computation.15.clone | custom fusion | bytes 540672 | tf_op jit(solution)/shard_map/jit(_take)/gather | solution.py:44
  353.8 3.6 broadcast_select_fusion.7
  358.0 3.6 broadcast_select_fusion.6
  362.3 3.6 broadcast_select_fusion.5
  366.5 3.6 broadcast_select_fusion.4
  370.8 3.6 broadcast_select_fusion.3
  374.4 1.3 copy.130
  375.8 3.6 broadcast_select_fusion.2
  379.4 1.3 copy.131
  380.7 3.6 broadcast_select_fusion.1
  384.3 1.3 copy.132
  385.7 3.9 broadcast_select_fusion
  389.7 1.3 copy.133
  391.1 2.7 fusion
  393.7 1.6 copy.115
  395.3 1.6 all_to_all.29
  397.1 12.4 %all_to_all.35 = f32[16,8,512]{2,0,1:T(8,128)S(1)} all-to-all(f32[16,8,512]{2,0,1:T(8,128)S(1)} %copy.116), channel_id=1, replica_groups=mesh['elem'=64,'mode'=8] {'mode'}, dimensions={1} | all-to-all | bytes 524288 | tf_op jit(solution)/shard_map/all_to_all | solution.py:81
  410.1 0.8 copy.117
  (153 shorter events, 11.2 us)
Async XLA Ops:
  0.0 1.0 copy-start
  0.0 20.0 %copy-start.23 = (f32[128]{0:T(128)S(1)}, f32[128]{0:T(128)}, u32[]{:S(2)}) copy-start(f32[128]{0:T(128)} %param.13) | copy-start | bytes 1540
  0.0 20.6 %copy-start.11 = (s32[256]{0:T(256)S(1)}, s32[256]{0:T(256)}, u32[]{:S(2)}) copy-start(s32[256]{0:T(256)} %param.16) | copy-start | bytes 3076
  2.9 18.4 %all-to-all-start = ((f32[8,16,512]{2,1,0:T(8,128)}), f32[8,16,512]{2,1,0:T(8,128)S(1)}, u32[]{:S(2)}, u32[]{:S(2)}) async-start(f32[8,16,512]{2,1,0:T(8,128)} %bitcast), calls=%async_computation | async-start | bytes 524288 | tf_op jit(solution)/shard_map/all_to_all | solution.py:69
  20.7 2.0 copy-start.12
  22.8 13.0 %collective-permute-start = (f32[16,16,128]{2,1,0:T(8,128)S(1)}, f32[16,16,128]{2,1,0:T(8,128)S(1)}, u32[]{:S(2)}, u32[]{:S(2)}) collective-permute-start(f32[16,16,128]{2,1,0:T(8,128)S(1)} %get-tuple-element.50), channel_id=1, source_target_pairs={{0,8},{8,16},{16,24},{24,32},{32,40},{40,48},{48,56},{56,64},{64,7... | collective-permute-start | bytes 393224 | tf_op jit(solution)/shard_map/ppermute | solution.py:13
  24.8 12.1 %collective-permute-start.1 = (f32[16,16,128]{2,1,0:T(8,128)S(1)}, f32[16,16,128]{2,1,0:T(8,128)S(1)}, u32[]{:S(2)}, u32[]{:S(2)}) collective-permute-start(f32[16,16,128]{2,1,0:T(8,128)S(1)} %get-tuple-element.51), channel_id=1, source_target_pairs={{8,0},{16,8},{24,16},{32,24},{40,32},{48,40},{56,48},{64,56},{72,6... | collective-permute-start | bytes 393224 | tf_op jit(solution)/shard_map/ppermute | solution.py:16
  120.9 17.6 %copy-start.3 = (pred[4096]{0:T(1024)(128)(4,1)S(1)}, pred[4096]{0:T(1024)(128)(4,1)}, u32[]{:S(2)}) copy-start(pred[4096]{0:T(1024)(128)(4,1)} %get-tuple-element.38) | copy-start | bytes 12292
  142.1 17.6 %copy-start.5 = (pred[4096]{0:T(1024)(128)(4,1)S(1)}, pred[4096]{0:T(1024)(128)(4,1)}, u32[]{:S(2)}) copy-start(pred[4096]{0:T(1024)(128)(4,1)} %get-tuple-element.40) | copy-start | bytes 12292
  163.3 17.6 %copy-start.7 = (pred[4096]{0:T(1024)(128)(4,1)S(1)}, pred[4096]{0:T(1024)(128)(4,1)}, u32[]{:S(2)}) copy-start(pred[4096]{0:T(1024)(128)(4,1)} %get-tuple-element.42) | copy-start | bytes 12292
  184.6 17.6 %copy-start.9 = (pred[4096]{0:T(1024)(128)(4,1)S(1)}, pred[4096]{0:T(1024)(128)(4,1)}, u32[]{:S(2)}) copy-start(pred[4096]{0:T(1024)(128)(4,1)} %get-tuple-element.44) | copy-start | bytes 12292
  209.7 10.5 %collective-permute-start.2 = (f32[16,16,128]{2,1,0:T(8,128)S(1)}, f32[16,16,128]{2,1,0:T(8,128)S(1)}, u32[]{:S(2)}, u32[]{:S(2)}) collective-permute-start(f32[16,16,128]{2,1,0:T(8,128)S(1)} %get-tuple-element.48), channel_id=1, source_target_pairs={{0,8},{8,16},{16,24},{24,32},{32,40},{40,48},{48,56},{56,64},{64,7... | collective-permute-start | bytes 393224 | tf_op jit(solution)/shard_map/ppermute | solution.py:13
  211.6 9.4 %collective-permute-start.3 = (f32[16,16,128]{2,1,0:T(8,128)S(1)}, f32[16,16,128]{2,1,0:T(8,128)S(1)}, u32[]{:S(2)}, u32[]{:S(2)}) collective-permute-start(f32[16,16,128]{2,1,0:T(8,128)S(1)} %get-tuple-element.49), channel_id=1, source_target_pairs={{8,0},{16,8},{24,16},{32,24},{40,32},{48,40},{56,48},{64,56},{72,6... | collective-permute-start | bytes 393224 | tf_op jit(solution)/shard_map/ppermute | solution.py:16
  370.1 0.7 copy-start.4
  374.4 1.3 copy-start.6
  379.4 1.3 copy-start.8
  384.3 1.3 copy-start.10
  389.5 1.4 copy-start.13
  389.5 1.4 copy-start.14
  389.6 1.4 copy-start.15
  389.6 1.4 copy-start.16
  389.6 1.4 copy-start.17
  389.6 1.4 copy-start.18
  389.6 1.4 copy-start.19
  389.6 1.4 copy-start.20
  389.6 1.4 copy-start.21
  389.6 1.4 copy-start.22
  389.6 1.4 copy-start.24
  389.6 1.4 copy-start.25
  393.7 17.2 %copy-start.1 = (f32[128,512]{1,0:T(8,128)S(1)}, f32[128,512]{1,0:T(8,128)}, u32[]{:S(2)}) copy-start(f32[128,512]{1,0:T(8,128)} %param.10) | copy-start | bytes 786436
  395.3 14.1 %copy-start.2 = (f32[128,128]{1,0:T(8,128)S(1)}, f32[128,128]{1,0:T(8,128)}, u32[]{:S(2)}) copy-start(f32[128,128]{1,0:T(8,128)} %param.12) | copy-start | bytes 196612
where the time goes:
time: 413 us; the launch traced here: 411 us
  local copies, waits for them, and re-layouts  290 us (70%)
  other arithmetic  64.9 us (16%)
  starting transfers between devices  31 us (8%)
  blocking collectives  12.4 us (3%)
  matrix products  7.73 us (2%)
    gather x16, local copies, waits for them, and re-layouts, schwarz_sweep(): jnp.take(flat, where_at.reshape(-1), axis=1).reshape(modes, 16, elems)  260 us
    select_n x16, other arithmetic, schwarz_sweep(): jnp.take(flat, where_at.reshape(-1), axis=1).reshape(modes, 16, elems)  58 us
    ppermute x2, starting transfers between devices, padded(): lax.ppermute(lax.slice_in_dim(block, 0, width, axis=dim), axis, backward)  17 us
    reshape x16, local copies, waits for them, and re-layouts, schwarz_sweep(): jnp.take(flat, where_at.reshape(-1), axis=1).reshape(modes, 16, elems)  16.3 us
    all_to_all x1, blocking collectives, body(): lax.all_to_all(u_flat, 'mode', split_axis=1, concat_axis=0, tiled=True)  12.4 us
    all_to_all x1, starting transfers between devices, body(): lax.all_to_all(all_modes, 'mode', split_axis=0, concat_axis=1, tiled=True)  10.2 us
  transfers between devices with their start and end apart: 5, of which 4 were waited for; matrix products, arithmetic and copies ran while one was open for 2% of the time, Pallas kernels for 0%

commit v1 on v0

v1 whole, which is shorter than its diff:
```python
import functools

import jax
import jax.numpy as jnp
from jax import lax
from jax.experimental import pallas as pl
from jax.experimental.pallas import tpu as pltpu
from jax.sharding import PartitionSpec as P


def split(x):
    high = x.astype(jnp.bfloat16)
    return high, (x - high.astype(jnp.float32)).astype(jnp.bfloat16)


def dot(a, b):
    return jnp.dot(a, b, preferred_element_type=jnp.float32)


def dot3(a, b):
    ah, al = split(a)
    bh, bl = split(b)
    return dot(ah, bh) + (dot(ah, bl) + dot(al, bh))


def to_modes_kernel(rhs_ref, modes_ref, scale_ref, out_ref):
    row = lax.broadcasted_iota(jnp.int32, (512, 512), 0)
    col = lax.broadcasted_iota(jnp.int32, (1, 512), 1)
    perm = (row == (col % 32) * 16 + col // 32).astype(jnp.float32).astype(jnp.bfloat16)
    high, low = split(rhs_ref[...])
    high = dot(high, perm).astype(jnp.bfloat16)
    low = dot(low, perm).astype(jnp.bfloat16)
    mh, ml = split(modes_ref[...])
    start = (dot(mh, high) + (dot(mh, low) + dot(ml, high))) * scale_ref[...]
    for group in range(8):
        for quad in range(4):
            part = start[16 * group : 16 * group + 16, 128 * quad : 128 * quad + 128]
            for copy in range(2):
                out_ref[8 * copy + group, 16 * quad : 16 * quad + 16, :] = part


def transpose_quads(parts):
    rows = parts[0].shape[0]
    where_at = lax.broadcasted_iota(jnp.int32, (rows, 128), 1) // 32
    outs = []
    for i in range(4):
        out = None
        for j in range(4):
            shift = (32 * (j - i)) % 128
            moved = parts[j] if shift == 0 else pltpu.roll(parts[j], shift, 1)
            out = moved if out is None else jnp.where(where_at == j, moved, out)
        outs.append(out)
    return outs


def half_table(tables, half, odd):
    even_at, odd_at = half + 2, 3 - half
    even_ref, odd_ref = tables[even_at // 2], tables[odd_at // 2]
    even_half, odd_half = even_at % 2, odd_at % 2
    even = even_ref[:, 128 * even_half : 128 * even_half + 128]
    other = odd_ref[:, 128 * odd_half : 128 * odd_half + 128]
    even_ids, other_ids = even[0:8], other[0:8]
    step = jnp.where(odd, 1 + odd_half - (other_ids >> 7), (even_ids >> 7) - 1 - even_half)
    both = jnp.where(odd, other, even)
    lane = both[0:8] & 127
    code = both[8:16]
    count = both[16:17]
    slot = lax.broadcasted_iota(jnp.int32, (8, 128), 0)
    step = jnp.where(slot < count, step, 9)
    return lane, step, code, 1.0 / count.astype(jnp.float32)


def gathered(src_ref, sources, table, row):
    lane, step, code, inv = table
    total = [jnp.zeros((8, 128), jnp.float32) for _ in range(16)]
    for k in range(8):
        spread = lambda x: jnp.broadcast_to(x[k : k + 1], (8, 128))
        lane_k, step_k, code_k = spread(lane), spread(step), spread(code)
        swap = (code_k & 1) == 1
        flip_row = (code_k & 2) == 2
        flip_col = (code_k & 4) == 4
        at = [step_k == d for d in sources]
        picked = []
        for p in range(16):
            value = jnp.zeros((8, 128), jnp.float32)
            for is_d, d in zip(at, sources):
                block = src_ref[sources[d], pl.ds(16 * p + row, 8), :]
                value = jnp.where(is_d, jnp.take_along_axis(block, lane_k, axis=1), value)
            picked.append(value)
        rows = [jnp.where(flip_row, picked[4 * (3 - i) + j], picked[4 * i + j]) for i in range(4) for j in range(4)]
        cols = [jnp.where(flip_col, rows[4 * i + 3 - j], rows[4 * i + j]) for i in range(4) for j in range(4)]
        for i in range(4):
            for j in range(4):
                p = 4 * i + j
                value = cols[p] if i == j else jnp.where(swap, cols[4 * j + i], cols[p])
                total[p] = total[p] + value
    return [t * inv for t in total]


def sweep_kernel(odd_ref, x_ref, before_ref, own_ref, after_ref, weight_ref, inverse_ref, out_ref, u_ref, w_ref, s_ref):
    odd = odd_ref[0] == 1
    tables = (before_ref, own_ref, after_ref)
    for half in range(4):
        base = 4 * jnp.where(odd, 3 - half, half)
        for quad in range(4):
            parts = [x_ref[base + j, 16 * quad : 16 * quad + 16, :] for j in range(4)]
            for i, part in enumerate(transpose_quads(parts)):
                u_ref[half, 64 * quad + 16 * i : 64 * quad + 16 * i + 16, :] = part
    inverse = inverse_ref[...]
    for place, half in enumerate((-1, 0, 1, 2)):
        table = half_table(tables, half, odd)
        sources = {d: half + d for d in (-1, 0, 1) if 0 <= half + d <= 3}

        def first(m, carry, place=place, table=table, sources=sources):
            row = pl.multiple_of(8 * m, 8)
            weight = weight_ref[pl.ds(row, 8), :]
            for p, value in enumerate(gathered(u_ref, sources, table, row)):
                s_ref[pl.ds(16 * p + row, 8), 128 * place : 128 * place + 128] = weight * value
            return carry

        lax.fori_loop(0, 2, first, 0)
    fixed = dot3(inverse, s_ref[...])
    for place in range(4):
        w_ref[place] = fixed[:, 128 * place : 128 * place + 128]
    for place, half in enumerate((-2, -1, 0, 1)):
        table = half_table(tables, half, odd)
        sources = {d: half + d + 1 for d in (-1, 0, 1) if 0 <= half + d + 1 <= 3}

        def second(m, carry, place=place, half=half, table=table, sources=sources):
            row = pl.multiple_of(8 * m, 8)
            weight = weight_ref[pl.ds(row, 8), :]
            for p, value in enumerate(gathered(w_ref, sources, table, row)):
                value = weight * value
                if half >= -1:
                    value = value - w_ref[half + 1, pl.ds(16 * p + row, 8), :]
                s_ref[pl.ds(16 * p + row, 8), 128 * place : 128 * place + 128] = value
            return carry

        lax.fori_loop(0, 2, second, 0)
    fixed = dot3(inverse, s_ref[...])
    for place, half in enumerate((-2, -1, 0, 1)):
        base = 4 * jnp.where(odd, 3 - place, place)
        for quad in range(4):
            parts = []
            for i in range(4):
                rows = slice(64 * quad + 16 * i, 64 * quad + 16 * i + 16)
                value = fixed[rows, 128 * place : 128 * place + 128]
                if half >= -1:
                    value = value + 2.0 * w_ref[half + 1, rows, :]
                if half >= 0:
                    value = value + u_ref[half, rows, :]
                parts.append(value)
            for j, part in enumerate(transpose_quads(parts)):
                out_ref[base + j, 16 * quad : 16 * quad + 16, :] = part


def to_levels_kernel(parts_ref, levels_ref, out_ref, modes_ref):
    for group in range(8):
        for quad in range(4):
            rows = slice(16 * quad, 16 * quad + 16)
            modes_ref[16 * group : 16 * group + 16, 128 * quad : 128 * quad + 128] = (
                parts_ref[group, rows, :] + parts_ref[8 + group, rows, :]
            )
    high, low = split(dot3(levels_ref[...], modes_ref[...]))
    row = lax.broadcasted_iota(jnp.int32, (512, 512), 0)
    col = lax.broadcasted_iota(jnp.int32, (1, 512), 1)
    perm = (row == (col % 16) * 32 + col // 16).astype(jnp.float32).astype(jnp.bfloat16)
    out_ref[...] = dot(high, perm) + dot(low, perm)


def shapes(*dims):
    return jax.ShapeDtypeStruct(dims, jnp.float32)


def cost(flops, moved):
    return pl.CostEstimate(flops=flops, bytes_accessed=moved, transcendentals=0)


def body(blocks, levels_rhs, to_modes, from_modes, helmholtz, local_inverse, neighbor_ids, neighbor_count, orientation):
    axes = ("elem", "mode")
    parts = lax.axis_size("mode")
    source_pairs = [[(2 * k + i) * parts + j for i in range(2) for j in range(parts)] for k in range(blocks // 2)]
    target_pairs = [
        [((2 * k - 1 + i) % blocks) * parts + j for i in range(2) for j in range(parts)] for k in range(blocks // 2)
    ]
    forward = [(i, (i + 1) % blocks) for i in range(blocks)]
    backward = [(b, a) for a, b in forward]

    table = jnp.concatenate([neighbor_ids, orientation, neighbor_count[None]], axis=0)
    before = lax.ppermute(table, "elem", forward)
    after = lax.ppermute(table, "elem", backward)

    start = pl.pallas_call(
        to_modes_kernel,
        out_shape=shapes(16, 64, 128),
        cost_estimate=cost(2 * 128 * 512 * (512 + 128), 1 << 20),
        name="to_modes_chunks",
    )(levels_rhs, to_modes, 1.0 / (1.0 + helmholtz)[:, None])
    sources = lax.all_to_all(start, axes, 0, 0, axis_index_groups=source_pairs, tiled=True)

    coeff = lax.dynamic_slice_in_dim(helmholtz, lax.axis_index("mode") * 16, 16, 0)
    weight = jnp.broadcast_to((coeff / (1.0 + coeff))[:, None], (16, 128))
    inverse = jnp.kron(local_inverse, jnp.eye(16, dtype=jnp.float32))
    odd = jnp.broadcast_to(lax.axis_index("elem") % 2, (1,)).astype(jnp.int32)
    vmem = pl.BlockSpec(memory_space=pltpu.VMEM)
    targets = pl.pallas_call(
        sweep_kernel,
        out_shape=shapes(16, 64, 128),
        in_specs=[pl.BlockSpec(memory_space=pltpu.SMEM)] + [vmem] * 6,
        out_specs=vmem,
        scratch_shapes=[
            pltpu.VMEM((4, 256, 128), jnp.float32),
            pltpu.VMEM((4, 256, 128), jnp.float32),
            pltpu.VMEM((256, 512), jnp.float32),
        ],
        cost_estimate=cost(1 << 30, 2 << 20),
        name="two_sweeps",
    )(odd, sources, before, table, after, weight, inverse)
    whole = lax.all_to_all(targets, axes, 0, 0, axis_index_groups=target_pairs, tiled=True)
    return pl.pallas_call(
        to_levels_kernel,
        out_shape=shapes(128, 512),
        scratch_shapes=[pltpu.VMEM((128, 512), jnp.float32)],
        cost_estimate=cost(2 * 128 * 512 * (512 + 128), 1 << 20),
        name="to_levels",
    )(whole, from_modes)


def solution(mesh):
    in_specs = (
        P(None, ("elem", "mode")),
        P(),
        P(),
        P(),
        P(),
        P(None, "elem"),
        P("elem"),
        P(None, "elem"),
    )
    out_specs = P(None, ("elem", "mode"))
    return jax.shard_map(
        functools.partial(body, mesh.shape["elem"]), mesh=mesh, in_specs=in_specs, out_specs=out_specs, check_vma=False
    )
```

time: 413 us -> 61.9 us (0.15)
  local copies, waits for them, and re-layouts: 290 us -> 3.08 us
  other arithmetic: 64.9 us -> 1.7 us
  Pallas kernels: 0 us -> 15.1 us
  starting transfers between devices: 31 us -> 22.4 us
  matrix products: 7.73 us -> 0 us
  blocking collectives: 12.4 us -> 19 us
    gather x16 -> x0, local copies, waits for them, and re-layouts: 260 us -> none  [schwarz_sweep(): jnp.take(flat, where_at.reshape(-1), axis=1).reshape(modes, 16, elems)]
    select_n x17 -> x0, other arithmetic: 58 us -> none  [the longest x16 58 us: schwarz_sweep(): jnp.take(flat, where_at.reshape(-1), axis=1).reshape(modes, 16, elems)]
    reshape x20 -> x0, local copies, waits for them, and re-layouts: 22.8 us -> none  [the longest x16 16.3 us: schwarz_sweep(): jnp.take(flat, where_at.reshape(-1), axis=1).reshape(modes, 16, elems)]
    pallas_call x0 -> x3, Pallas kernels: none -> 15.1 us  [the longest x1 10.4 us: body(): pl.pallas_call(sweep_kernel, out_shape=shapes(16, 64, 128), in_specs=[pl....]
    ppermute x4 -> x2, starting transfers between devices: 20.9 us -> 12.2 us  [the longest x1 8.84 us: body(): after = lax.ppermute(table, 'elem', backward)]
    dot_general x4 -> x0, matrix products: 7.73 us -> none  [the longest x2 5.24 us: schwarz_sweep(): jnp.einsum('pq,mqe->mpe', local_inverse, resid, precision=lax.Precision.H...]
    all_to_all x1, blocking collectives: 12.4 us -> 19 us  [body(): lax.all_to_all(targets, axes, 0, 0, axis_index_groups=target_pairs, tiled...]
  transfers between devices with their start and end apart: 5 -> 3, of which waited for: 4 -> 0; matrix products, arithmetic and copies ran while one was open for 2% -> 4% of each run, Pallas kernels for 0% -> 0%
where the time goes in v1:
time: 61.9 us; the launch traced here: 61.4 us
  starting transfers between devices  22.4 us (36%)
  blocking collectives  19 us (31%)
  Pallas kernels  15.1 us (24%)
  local copies, waits for them, and re-layouts  3.08 us (5%)
  other arithmetic  1.7 us (3%)
    all_to_all x1, blocking collectives, body(): lax.all_to_all(targets, axes, 0, 0, axis_index_groups=target_pairs, tiled...  19 us
    pallas_call x1, Pallas kernels, body(): pl.pallas_call(sweep_kernel, out_shape=shapes(16, 64, 128), in_specs=[pl....  10.4 us
    all_to_all x1, starting transfers between devices, body(): lax.all_to_all(start, axes, 0, 0, axis_index_groups=source_pairs, tiled=T...  10.2 us
    ppermute x1, starting transfers between devices, body(): after = lax.ppermute(table, 'elem', backward)  8.84 us
    ppermute x1, starting transfers between devices, body(): before = lax.ppermute(table, 'elem', forward)  3.33 us
    pallas_call x1, Pallas kernels, body(): pl.pallas_call(to_modes_kernel, out_shape=shapes(16, 64, 128), cost_estim...  2.4 us
    pallas_call x1, Pallas kernels, body(): pl.pallas_call(to_levels_kernel, out_shape=shapes(128, 512), scratch_shap...  2.3 us
    mul x1, local copies, waits for them, and re-layouts, body(): inverse = jnp.kron(local_inverse, jnp.eye(16, dtype=jnp.float32))  1.54 us
  transfers between devices with their start and end apart: 3, of which 0 were waited for; matrix products, arithmetic and copies ran while one was open for 4% of the time, Pallas kernels for 0%

profile of v1, /device:TPU:1, one launch (start us, length us, event | category | flops | bytes accessed | tf_op | source)
XLA Modules:
  0.0 61.4 jit_solution(15612686319040445007)
XLA Ops:
  0.0 0.0 copy-start.2
  0.0 0.7 %divide_bitcast_fusion = f32[128,1]{0,1:T(1,128)S(1)} fusion(f32[128]{0:T(128)} %param.11), kind=kLoop, calls=%fused_computation.5 | loop fusion | flops 256 | bytes 1024 | tf_op jit(solution)/shard_map/div | solution.py:198
  0.7 0.0 copy-start.5
  0.7 0.7 %copy.9.scale_ref = f32[128,1]{1,0:T(8,128)} copy(f32[128,1]{0,1:T(1,128)S(1)} %divide_bitcast_fusion) | data formatting | bytes 1024 | tf_op jit(solution)/shard_map/div | solution.py:198
  1.4 2.4 %to_modes_chunks.1 = f32[16,64,128]{2,1,0:T(8,128)} custom-call(f32[128,512]{1,0:T(8,128)} %rhs_ref.1, f32[128,128]{1,0:T(8,128)} %modes_ref.1, f32[128,1]{1,0:T(8,128)} %copy.9.scale_ref), custom_call_target="tpu_custom_call" | custom-call | flops 83886080 | bytes 1048576 | tf_op jit(solution)/shard_map/to_modes_chunks/pallas_call | solution.py:193
  3.8 10.2 %all-to-all-start = ((f32[16,64,128]{2,1,0:T(8,128)}), f32[16,64,128]{2,1,0:T(8,128)S(1)}, u32[]{:S(2)}, u32[]{:S(2)}) async-start(f32[16,64,128]{2,1,0:T(8,128)} %to_modes_chunks.1), calls=%async_computation | async-start | bytes 1048576 | tf_op jit(solution)/shard_map/all_to_all | solution.py:199
  14.1 0.7 %pad_add_fusion.own_ref = s32[17,256]{1,0:T(8,128)S(1)} fusion(s32[1,256]{1,0:T(1,128)} %bitcast.6, s32[8,256]{1,0:T(8,128)} %param.15, s32[8,256]{1,0:T(8,128)} %param.13), kind=kLoop, calls=%fused_computation.1 | loop fusion | flops 8704 | bytes 34816 | tf_op jit(solution)/shard_map/concatenate | solution.py:189
  14.8 0.0 copy-start.1
  14.8 3.3 %collective-permute-start = (s32[17,256]{1,0:T(8,128)S(1)}, s32[17,256]{1,0:T(8,128)S(1)}, u32[]{:S(2)}, u32[]{:S(2)}) collective-permute-start(s32[17,256]{1,0:T(8,128)S(1)} %pad_add_fusion.own_ref), channel_id=1, source_target_pairs={{0,8},{8,16},{16,24},{24,32},{32,40},{40,48},{48,56},{56,64},{64,7... | collective-permute-start | bytes 52232 | tf_op jit(solution)/shard_map/ppermute | solution.py:190
  18.1 8.8 %collective-permute-start.1 = (s32[17,256]{1,0:T(8,128)S(1)}, s32[17,256]{1,0:T(8,128)S(1)}, u32[]{:S(2)}, u32[]{:S(2)}) collective-permute-start(s32[17,256]{1,0:T(8,128)S(1)} %pad_add_fusion.own_ref), channel_id=1, source_target_pairs={{8,0},{16,8},{24,16},{32,24},{40,32},{48,40},{56,48},{64,56},{72,6... | collective-permute-start | bytes 52232 | tf_op jit(solution)/shard_map/ppermute | solution.py:191
  27.0 0.0 copy-done.2
  27.0 0.2 broadcast_multiply_fusion
  27.2 0.0 copy-done.5
  27.2 0.1 add_divide_fusion
  27.3 1.5 %mul.31.inverse_ref = f32[256,256]{1,0:T(8,128)} reshape(f32[16,16,16,16]{3,2,1,0:T(8,128)S(1)} %broadcast_multiply_fusion) | data formatting | bytes 524288 | tf_op jit(solution)/shard_map/jit(kron)/mul | solution.py:203
  28.9 0.0 copy-done.1
  28.9 0.0 collective-permute-done.before_ref
  28.9 0.0 copy-start.3
  28.9 0.0 collective-permute-done.1.after_ref
  28.9 0.0 copy-start.4
  28.9 0.0 all-to-all-done.x_ref
  28.9 0.0 copy-start
  28.9 0.8 %broadcast_in_dim.19.weight_ref = f32[16,128]{1,0:T(8,128)} broadcast(f32[16]{0:T(128)S(1)} %add_divide_fusion), dimensions={0} | broadcast | bytes 8256 | tf_op jit(solution)/shard_map/broadcast_in_dim | solution.py:202
  29.7 0.0 copy-done.3
  29.7 0.0 copy-done.4
  29.7 0.0 copy-done
  29.7 10.4 %two_sweeps.1 = f32[16,64,128]{2,1,0:T(8,128)} custom-call(s32[1]{0:T(128)} %bitcast.odd_ref, f32[16,64,128]{2,1,0:T(8,128)} %copy-done, s32[17,256]{1,0:T(8,128)} %copy-done.3, s32[17,256]{1,0:T(8,128)} %copy-done.1, s32[17,256]{1,0:T(8,128)} %copy-done.4, f32[16,128]{1,0:T(8,128)} %broadcast_in_dim.19.weight_ref, f32[256,256]{1,0:T(8,128)} %mul.31.inverse_ref), custom_call_target="tpu_custom_call" | custom-call | flops 1073741824 | bytes 2097152 | tf_op jit(solution)/shard_map/two_sweeps/pallas_call | solution.py:206
  40.1 19.0 %all_to_all.10.parts_ref = f32[16,64,128]{2,1,0:T(8,128)} all-to-all(f32[16,64,128]{2,1,0:T(8,128)} %two_sweeps.1), channel_id=1, replica_groups={{504,505,506,507,508,509,510,511,0,1,2,3,4,5,6,7},{8,9,10,11,12,13,14,1..., dimensions={0} | all-to-all | bytes 1048576 | tf_op jit(solution)/shard_map/all_to_all | solution.py:219
  59.1 2.3 %to_levels.1 = f32[128,512]{1,0:T(8,128)} custom-call(f32[16,64,128]{2,1,0:T(8,128)} %all_to_all.10.parts_ref, f32[128,128]{1,0:T(8,128)} %levels_ref.1), custom_call_target="tpu_custom_call" | custom-call | flops 83886080 | bytes 1048576 | tf_op jit(solution)/shard_map/to_levels/pallas_call | solution.py:220
  (1 shorter events, 0.0 us)
Async XLA Ops:
  0.0 27.0 %copy-start.2 = (f32[16,16]{1,0:T(8,128)S(1)}, f32[16,16]{1,0:T(8,128)}, u32[]{:S(2)}) copy-start(f32[16,16]{1,0:T(8,128)} %param.12) | copy-start | bytes 3076
  0.7 26.5 %copy-start.5 = (f32[128]{0:T(128)S(1)}, f32[128]{0:T(128)}, u32[]{:S(2)}) copy-start(f32[128]{0:T(128)} %param.11) | copy-start | bytes 1540
  3.8 25.1 %all-to-all-start = ((f32[16,64,128]{2,1,0:T(8,128)}), f32[16,64,128]{2,1,0:T(8,128)S(1)}, u32[]{:S(2)}, u32[]{:S(2)}) async-start(f32[16,64,128]{2,1,0:T(8,128)} %to_modes_chunks.1), calls=%async_computation | async-start | bytes 1048576 | tf_op jit(solution)/shard_map/all_to_all | solution.py:199
  14.8 14.1 %copy-start.1 = (s32[17,256]{1,0:T(8,128)}, s32[17,256]{1,0:T(8,128)S(1)}, u32[]{:S(2)}) copy-start(s32[17,256]{1,0:T(8,128)S(1)} %pad_add_fusion.own_ref) | copy-start | bytes 52228
  14.8 14.1 %collective-permute-start = (s32[17,256]{1,0:T(8,128)S(1)}, s32[17,256]{1,0:T(8,128)S(1)}, u32[]{:S(2)}, u32[]{:S(2)}) collective-permute-start(s32[17,256]{1,0:T(8,128)S(1)} %pad_add_fusion.own_ref), channel_id=1, source_target_pairs={{0,8},{8,16},{16,24},{24,32},{32,40},{40,48},{48,56},{56,64},{64,7... | collective-permute-start | bytes 52232 | tf_op jit(solution)/shard_map/ppermute | solution.py:190
  18.1 10.7 %collective-permute-start.1 = (s32[17,256]{1,0:T(8,128)S(1)}, s32[17,256]{1,0:T(8,128)S(1)}, u32[]{:S(2)}, u32[]{:S(2)}) collective-permute-start(s32[17,256]{1,0:T(8,128)S(1)} %pad_add_fusion.own_ref), channel_id=1, source_target_pairs={{8,0},{16,8},{24,16},{32,24},{40,32},{48,40},{56,48},{64,56},{72,6... | collective-permute-start | bytes 52232 | tf_op jit(solution)/shard_map/ppermute | solution.py:191
  28.9 0.8 %copy-start.3 = (s32[17,256]{1,0:T(8,128)}, s32[17,256]{1,0:T(8,128)S(1)}, u32[]{:S(2)}) copy-start(s32[17,256]{1,0:T(8,128)S(1)} %collective-permute-done.before_ref) | copy-start | bytes 52228
  28.9 0.8 %copy-start.4 = (s32[17,256]{1,0:T(8,128)}, s32[17,256]{1,0:T(8,128)S(1)}, u32[]{:S(2)}) copy-start(s32[17,256]{1,0:T(8,128)S(1)} %collective-permute-done.1.after_ref) | copy-start | bytes 52228
  28.9 0.8 %copy-start = (f32[16,64,128]{2,1,0:T(8,128)}, f32[16,64,128]{2,1,0:T(8,128)S(1)}, u32[]{:S(2)}) copy-start(f32[16,64,128]{2,1,0:T(8,128)S(1)} %all-to-all-done.x_ref) | copy-start | bytes 1572868

commit v2 on v1

v2 whole, which is shorter than its diff:
```python
import functools

import jax
import jax.numpy as jnp
from jax import lax
from jax.experimental import pallas as pl
from jax.experimental.pallas import tpu as pltpu
from jax.sharding import PartitionSpec as P


def split(x):
    high = x.astype(jnp.bfloat16)
    return high, (x - high.astype(jnp.float32)).astype(jnp.bfloat16)


def dot(a, b):
    return jnp.dot(a, b, preferred_element_type=jnp.float32)


def dot3(a, b):
    ah, al = split(a)
    bh, bl = split(b)
    return dot(ah, bh) + (dot(ah, bl) + dot(al, bh))


def column(row):
    count = row.shape[1]
    at = lax.broadcasted_iota(jnp.int32, (count, count), 0) == lax.broadcasted_iota(jnp.int32, (count, count), 1)
    return jnp.sum(jnp.where(at, row, 0.0), axis=1, keepdims=True)


def fetch(pairs, sems):
    copies = [pltpu.make_async_copy(src, dst, sems.at[i]) for i, (src, dst) in enumerate(pairs)]
    for copy in copies:
        copy.start()
    return copies


def to_modes_kernel(
    rhs_hbm, modes_hbm, helmholtz_hbm, ids_hbm, orientation_hbm, count_hbm,
    out_ref, table_ref, rhs_ref, modes_ref, helmholtz_ref, count_ref, sems,
):
    copies = fetch(
        (
            (rhs_hbm, rhs_ref),
            (modes_hbm, modes_ref),
            (helmholtz_hbm, helmholtz_ref),
            (ids_hbm, table_ref.at[0:8]),
            (orientation_hbm, table_ref.at[8:16]),
            (count_hbm, count_ref),
        ),
        sems,
    )
    row = lax.broadcasted_iota(jnp.int32, (512, 512), 0)
    col = lax.broadcasted_iota(jnp.int32, (1, 512), 1)
    perm = (row == (col % 32) * 16 + col // 32).astype(jnp.float32).astype(jnp.bfloat16)
    for copy in copies:
        copy.wait()
    table_ref[16:24] = jnp.broadcast_to(count_ref[...], (8, 256))
    high, low = split(rhs_ref[...])
    high = dot(high, perm).astype(jnp.bfloat16)
    low = dot(low, perm).astype(jnp.bfloat16)
    mh, ml = split(modes_ref[...] * column(1.0 / (1.0 + helmholtz_ref[...])))
    start = dot(mh, high) + (dot(mh, low) + dot(ml, high))
    for group in range(8):
        for quad in range(4):
            part = start[16 * group : 16 * group + 16, 128 * quad : 128 * quad + 128]
            for copy in range(2):
                out_ref[8 * copy + group, 16 * quad : 16 * quad + 16, :] = part


def transpose_quads(parts):
    rows = parts[0].shape[0]
    where_at = lax.broadcasted_iota(jnp.int32, (rows, 128), 1) // 32
    outs = []
    for i in range(4):
        out = None
        for j in range(4):
            shift = (32 * (j - i)) % 128
            moved = parts[j] if shift == 0 else pltpu.roll(parts[j], shift, 1)
            out = moved if out is None else jnp.where(where_at == j, moved, out)
        outs.append(out)
    return outs


REACH = {-2: (1,), -1: (0, 1), 0: (-1, 0, 1), 1: (-1, 0, 1), 2: (-1, 0, 1)}
OWN = {0: 0, 1: 3}
OTHER = {-2: 0, -1: 1, 2: 3}


def half_table(table_ref, half, odd):
    even_half, odd_half = half % 2, (half + 1) % 2
    even = table_ref[:, 128 * even_half : 128 * even_half + 128]
    other = table_ref[:, 128 * odd_half : 128 * odd_half + 128]
    step = jnp.where(odd, 1 + odd_half - (other[0:8] >> 7), (even[0:8] >> 7) - 1 - even_half)
    both = jnp.where(odd, other, even)
    count = both[16:24]
    slot = lax.broadcasted_iota(jnp.int32, (8, 128), 0)
    return both[0:8] & 127, jnp.where(slot < count, step, 9), both[8:16], 1.0 / count[0:1].astype(jnp.float32)


def write_picks(table_ref, half, odd, pick_ref, at):
    lane, step, code, inv = half_table(table_ref, half, odd)
    source = lax.broadcasted_iota(jnp.int32, (128, 128), 0)
    for i, d in enumerate(REACH[half]):
        wanted = jnp.where(step == d, lane, -1)
        for k in range(8):
            pick = (source == wanted[k : k + 1]).astype(jnp.float32).astype(jnp.bfloat16)
            pick_ref[k // 2, at + i, :, 128 * (k % 2) : 128 * (k % 2) + 128] = pick
    return code, inv


def tables_kernel(
    place_ref, own_ref, helmholtz_hbm, inverse_hbm,
    pick_ref, code_ref, weight_ref, inv_ref, high_ref, low_ref, again_ref, helmholtz_ref, inverse_ref, sems,
):
    again_ref[...] = own_ref[...]
    copies = fetch(((helmholtz_hbm, helmholtz_ref), (inverse_hbm, inverse_ref)), sems)
    odd = place_ref[0] == 1
    for half in (0, 1):
        code, inv = write_picks(own_ref, half, odd, pick_ref, 3 * half)
        code_ref[half] = code
        inv_ref[half] = jnp.broadcast_to(inv, (8, 128))
    for copy in copies:
        copy.wait()
    rows = lax.broadcasted_iota(jnp.int32, (16, 128), 0)
    lanes = lax.broadcasted_iota(jnp.int32, (16, 128), 1)
    coeff = jnp.sum(jnp.where(lanes == rows + 16 * place_ref[1], helmholtz_ref[...], 0.0), axis=1, keepdims=True)
    weight_ref[...] = jnp.broadcast_to(coeff / (1.0 + coeff), (16, 128))
    big = lax.broadcasted_iota(jnp.int32, (256, 16), 0) // 16 == lax.broadcasted_iota(jnp.int32, (256, 16), 1)
    rise = big.astype(jnp.float32).astype(jnp.bfloat16)
    wide = lax.broadcasted_iota(jnp.int32, (16, 256), 1) // 16 == lax.broadcasted_iota(jnp.int32, (16, 256), 0)
    spread = wide.astype(jnp.float32).astype(jnp.bfloat16)
    same = (
        lax.broadcasted_iota(jnp.int32, (256, 256), 0) % 16 == lax.broadcasted_iota(jnp.int32, (256, 256), 1) % 16
    )
    for ref, part in zip((high_ref, low_ref), split(inverse_ref[...])):
        ref[...] = jnp.where(same, dot(dot(rise, part).astype(jnp.bfloat16), spread), 0.0).astype(jnp.bfloat16)


def neighbor_sum(split_ref, first, count, pick_ref, at, code):
    total = [[None] * 16 for _ in range(2)]
    lhs = split_ref[:, 256 * first : 256 * (first + count)]
    for pair in range(4):
        rhs = jnp.concatenate([pick_ref[pair, at + c // 2] for c in range(2 * count)], axis=0)
        found = dot(lhs, rhs)
        for side in range(2):
            code_k = jnp.broadcast_to(code[2 * pair + side : 2 * pair + side + 1], (8, 128))
            swap = (code_k & 1) == 1
            flip_row = (code_k & 2) == 2
            flip_col = (code_k & 4) == 4
            for m in range(2):
                x = [found[16 * p + 8 * m : 16 * p + 8 * m + 8, 128 * side : 128 * side + 128] for p in range(16)]
                x = [jnp.where(flip_row, x[4 * (3 - i) + j], x[4 * i + j]) for i in range(4) for j in range(4)]
                x = [jnp.where(flip_col, x[4 * i + 3 - j], x[4 * i + j]) for i in range(4) for j in range(4)]
                x = [x[5 * i] if i == j else jnp.where(swap, x[4 * j + i], x[4 * i + j]) for i in range(4) for j in range(4)]
                total[m] = [v if t is None else t + v for t, v in zip(total[m], x)]
    return total


def fix(high_ref, low_ref, x):
    xh, xl = split(x)
    return dot(high_ref[...], xh) + (dot(high_ref[...], xl) + dot(low_ref[...], xh))


def sweep_kernel(
    place_ref, x_ref, source_table_ref, target_table_ref, pick_ref, code_ref, weight_ref, inv_ref, high_ref, low_ref,
    out_ref, u_ref, w_ref, us_ref, ws_ref, s_ref, other_ref,
):
    odd = place_ref[0] == 1
    known = {half: (code_ref[half], inv_ref[half]) for half in OWN}
    for half in OTHER:
        table_ref = source_table_ref if half == 2 else target_table_ref
        known[half] = write_picks(table_ref, half, odd, other_ref, OTHER[half])
    for half in range(4):
        base = 4 * jnp.where(odd, 3 - half, half)
        for quad in range(4):
            parts = [x_ref[base + j, 16 * quad : 16 * quad + 16, :] for j in range(4)]
            for i, part in enumerate(transpose_quads(parts)):
                rows = slice(64 * quad + 16 * i, 64 * quad + 16 * i + 16)
                u_ref[half, rows, :] = part
                high, low = split(part)
                us_ref[rows, 256 * half : 256 * half + 128] = high
                us_ref[rows, 256 * half + 128 : 256 * half + 256] = low
    for place, half in enumerate((-1, 0, 1, 2)):
        steps = [d for d in REACH[half] if 0 <= half + d <= 3]
        picks, at = (pick_ref, OWN[half]) if half in OWN else (other_ref, OTHER[half])
        code, inv = known[half]
        total = neighbor_sum(us_ref, half + steps[0], len(steps), picks, at + REACH[half].index(steps[0]), code)
        for m in range(2):
            weight = weight_ref[8 * m : 8 * m + 8, :] * inv
            for p in range(16):
                s_ref[16 * p + 8 * m : 16 * p + 8 * m + 8, 128 * place : 128 * place + 128] = weight * total[m][p]
    fixed = fix(high_ref, low_ref, s_ref[...])
    for place in range(4):
        part = fixed[:, 128 * place : 128 * place + 128]
        w_ref[place] = part
        high, low = split(part)
        ws_ref[:, 256 * place : 256 * place + 128] = high
        ws_ref[:, 256 * place + 128 : 256 * place + 256] = low
    for place, half in enumerate((-2, -1, 0, 1)):
        steps = [d for d in REACH[half] if -1 <= half + d <= 2]
        picks, at = (pick_ref, OWN[half]) if half in OWN else (other_ref, OTHER[half])
        code, inv = known[half]
        total = neighbor_sum(ws_ref, half + steps[0] + 1, len(steps), picks, at + REACH[half].index(steps[0]), code)
        for m in range(2):
            weight = weight_ref[8 * m : 8 * m + 8, :] * inv
            for p in range(16):
                rows = slice(16 * p + 8 * m, 16 * p + 8 * m + 8)
                value = weight * total[m][p]
                if half >= -1:
                    value = value - w_ref[half + 1, rows, :]
                s_ref[rows, 128 * place : 128 * place + 128] = value
    fixed = fix(high_ref, low_ref, s_ref[...])
    for place, half in enumerate((-2, -1, 0, 1)):
        base = 4 * jnp.where(odd, 3 - place, place)
        for quad in range(4):
            parts = []
            for i in range(4):
                rows = slice(64 * quad + 16 * i, 64 * quad + 16 * i + 16)
                value = fixed[rows, 128 * place : 128 * place + 128]
                if half >= -1:
                    value = value + 2.0 * w_ref[half + 1, rows, :]
                if half >= 0:
                    value = value + u_ref[half, rows, :]
                parts.append(value)
            for j, part in enumerate(transpose_quads(parts)):
                out_ref[base + j, 16 * quad : 16 * quad + 16, :] = part


def to_levels_kernel(parts_ref, levels_ref, out_ref, modes_ref):
    for group in range(8):
        for quad in range(4):
            rows = slice(16 * quad, 16 * quad + 16)
            modes_ref[16 * group : 16 * group + 16, 128 * quad : 128 * quad + 128] = (
                parts_ref[group, rows, :] + parts_ref[8 + group, rows, :]
            )
    high, low = split(dot3(levels_ref[...], modes_ref[...]))
    row = lax.broadcasted_iota(jnp.int32, (512, 512), 0)
    col = lax.broadcasted_iota(jnp.int32, (1, 512), 1)
    perm = (row == (col % 16) * 32 + col // 16).astype(jnp.float32).astype(jnp.bfloat16)
    out_ref[...] = dot(high, perm) + dot(low, perm)


def cost(flops, moved):
    return pl.CostEstimate(flops=flops, bytes_accessed=moved, transcendentals=0)


def near(x):
    return pltpu.with_memory_space_constraint(x, pltpu.VMEM)


def far(x):
    return pltpu.with_memory_space_constraint(x, pltpu.HBM)


VMEM = pl.BlockSpec(memory_space=pltpu.VMEM)
SMEM = pl.BlockSpec(memory_space=pltpu.SMEM)
HBM = pl.BlockSpec(memory_space=pltpu.HBM)
LIMIT = pltpu.CompilerParams(vmem_limit_bytes=20 << 20)


def body(blocks, levels_rhs, to_modes, from_modes, helmholtz, local_inverse, neighbor_ids, neighbor_count, orientation):
    axes = ("elem", "mode")
    parts = lax.axis_size("mode")
    source_pairs = [[(2 * k + i) * parts + j for i in range(2) for j in range(parts)] for k in range(blocks // 2)]
    target_pairs = [
        [((2 * k - 1 + i) % blocks) * parts + j for i in range(2) for j in range(parts)] for k in range(blocks // 2)
    ]
    source_swap = [(b, b ^ 1) for b in range(blocks)]
    target_swap = [(b, (((b + 1) ^ 1) - 1) % blocks) for b in range(blocks)]
    helmholtz = helmholtz[None]
    place = jnp.stack([lax.axis_index("elem") % 2, lax.axis_index("mode")]).astype(jnp.int32)

    start, own = pl.pallas_call(
        to_modes_kernel,
        out_shape=(pltpu.VMEM((16, 64, 128), jnp.float32), pltpu.VMEM((24, 256), jnp.int32)),
        in_specs=[HBM] * 6,
        out_specs=(VMEM, VMEM),
        scratch_shapes=[
            pltpu.VMEM((128, 512), jnp.float32),
            pltpu.VMEM((128, 128), jnp.float32),
            pltpu.VMEM((1, 128), jnp.float32),
            pltpu.VMEM((1, 256), jnp.int32),
            pltpu.SemaphoreType.DMA((6,)),
        ],
        compiler_params=LIMIT,
        cost_estimate=cost(2 * 128 * 512 * (512 + 128), 1 << 20),
        name="to_modes_chunks",
    )(*[far(x) for x in (levels_rhs, to_modes, helmholtz, neighbor_ids, orientation, neighbor_count[None])])
    sources = lax.all_to_all(start, axes, 0, 0, axis_index_groups=source_pairs, tiled=True)
    source_table = lax.ppermute(own, "elem", source_swap)
    *parts_of_tables, again = pl.pallas_call(
        tables_kernel,
        out_shape=(
            pltpu.VMEM((4, 6, 128, 256), jnp.bfloat16),
            pltpu.VMEM((2, 8, 128), jnp.int32),
            pltpu.VMEM((16, 128), jnp.float32),
            pltpu.VMEM((2, 8, 128), jnp.float32),
            pltpu.VMEM((256, 256), jnp.bfloat16),
            pltpu.VMEM((256, 256), jnp.bfloat16),
            pltpu.VMEM((24, 256), jnp.int32),
        ),
        in_specs=[SMEM, VMEM, HBM, HBM],
        out_specs=(VMEM,) * 7,
        scratch_shapes=[
            pltpu.VMEM((1, 128), jnp.float32),
            pltpu.VMEM((16, 16), jnp.float32),
            pltpu.SemaphoreType.DMA((2,)),
        ],
        compiler_params=LIMIT,
        cost_estimate=cost(1 << 28, 2 << 20),
        name="own_tables",
    )(place, near(own), far(helmholtz), far(local_inverse))
    target_table = lax.ppermute(again, "elem", target_swap)
    targets = pl.pallas_call(
        sweep_kernel,
        out_shape=pltpu.VMEM((16, 64, 128), jnp.float32),
        in_specs=[SMEM] + [VMEM] * 9,
        out_specs=VMEM,
        scratch_shapes=[
            pltpu.VMEM((4, 256, 128), jnp.float32),
            pltpu.VMEM((4, 256, 128), jnp.float32),
            pltpu.VMEM((256, 1024), jnp.bfloat16),
            pltpu.VMEM((256, 1024), jnp.bfloat16),
            pltpu.VMEM((256, 512), jnp.float32),
            pltpu.VMEM((4, 6, 128, 256), jnp.bfloat16),
        ],
        compiler_params=LIMIT,
        cost_estimate=cost(4 << 30, 8 << 20),
        name="two_sweeps",
    )(place, near(sources), near(source_table), near(target_table), *[near(part) for part in parts_of_tables])
    whole = lax.all_to_all(targets, axes, 0, 0, axis_index_groups=target_pairs, tiled=True)
    return pl.pallas_call(
        to_levels_kernel,
        out_shape=jax.ShapeDtypeStruct((128, 512), jnp.float32),
        in_specs=[VMEM] * 2,
        out_specs=VMEM,
        scratch_shapes=[pltpu.VMEM((128, 512), jnp.float32)],
        compiler_params=LIMIT,
        cost_estimate=cost(2 * 128 * 512 * (512 + 128), 1 << 20),
        name="to_levels",
    )(near(whole), from_modes)


def solution(mesh):
    in_specs = (
        P(None, ("elem", "mode")),
        P(),
        P(),
        P(),
        P(),
        P(None, "elem"),
        P("elem"),
        P(None, "elem"),
    )
    out_specs = P(None, ("elem", "mode"))
    return jax.shard_map(
        functools.partial(body, mesh.shape["elem"]), mesh=mesh, in_specs=in_specs, out_specs=out_specs, check_vma=False
    )
```

time: 61.9 us -> 54 us (0.87)
  Pallas kernels: 15.1 us -> 9.98 us
  local copies, waits for them, and re-layouts: 3.08 us -> 0.01 us
  other arithmetic: 1.7 us -> 0.08 us
  waiting for transfers between devices: 0.01 us -> 1.2 us
  blocking collectives: 19 us -> 19.9 us
    pallas_call x3 -> x4, Pallas kernels: 15.1 us -> 9.98 us  [the longest x1 4.79 us: body(): pl.pallas_call(sweep_kernel, out_shape=pltpu.VMEM((16, 64, 128), jnp.floa...]
    mul x1 -> x0, local copies, waits for them, and re-layouts: 1.54 us -> none  [body(): inverse = jnp.kron(local_inverse, jnp.eye(16, dtype=jnp.float32))]
    ppermute x2, waiting for transfers between devices: 0.01 us -> 1.19 us  [the longest x1 1.19 us: body(): target_table = lax.ppermute(again, 'elem', target_swap)]
    all_to_all x1, blocking collectives: 19 us -> 19.9 us  [body(): lax.all_to_all(targets, axes, 0, 0, axis_index_groups=target_pairs, tiled...]
    broadcast_in_dim x1 -> x0, local copies, waits for them, and re-layouts: 0.77 us -> none  [body(): weight = jnp.broadcast_to((coeff / (1.0 + coeff))[:, None], (16, 128))]
    div x2 -> x0, other arithmetic: 0.75 us -> none  [the longest x1 0.67 us: body(): 1.0 / (1.0 + helmholtz)[:, None]]
    div x1 -> x0, local copies, waits for them, and re-layouts: 0.75 us -> none  [body(): 1.0 / (1.0 + helmholtz)[:, None]]
    concatenate x1 -> x0, other arithmetic: 0.73 us -> none  [body(): jnp.concatenate([neighbor_ids, orientation, neighbor_count[None]], axis=0)]
  transfers between devices with their start and end apart: 3 -> 3, of which waited for: 0 -> 1; matrix products, arithmetic and copies ran while one was open for 4% -> 0% of each run, Pallas kernels for 0% -> 3%
where the time goes in v2:
time: 54 us; the launch traced here: 53.7 us
  starting transfers between devices  22.5 us (42%)
  blocking collectives  19.9 us (37%)
  Pallas kernels  9.98 us (18%)
  waiting for transfers between devices  1.2 us (2%)
    all_to_all x1, blocking collectives, body(): lax.all_to_all(targets, axes, 0, 0, axis_index_groups=target_pairs, tiled...  19.9 us
    all_to_all x1, starting transfers between devices, body(): lax.all_to_all(start, axes, 0, 0, axis_index_groups=source_pairs, tiled=T...  10.2 us
    ppermute x1, starting transfers between devices, body(): target_table = lax.ppermute(again, 'elem', target_swap)  8.95 us
    pallas_call x1, Pallas kernels, body(): pl.pallas_call(sweep_kernel, out_shape=pltpu.VMEM((16, 64, 128), jnp.floa...  4.79 us
    ppermute x1, starting transfers between devices, body(): source_table = lax.ppermute(own, 'elem', source_swap)  3.33 us
    pallas_call x1, Pallas kernels, body(): pl.pallas_call(to_modes_kernel, out_shape=(pltpu.VMEM((16, 64, 128), jnp....  2.34 us
    pallas_call x1, Pallas kernels, body(): pl.pallas_call(tables_kernel, out_shape=(pltpu.VMEM((4, 6, 128, 256), jnp...  1.6 us
    pallas_call x1, Pallas kernels, body(): pl.pallas_call(to_levels_kernel, out_shape=jax.ShapeDtypeStruct((128, 512...  1.26 us
  transfers between devices with their start and end apart: 3, of which 1 were waited for; matrix products, arithmetic and copies ran while one was open for 0% of the time, Pallas kernels for 3%

profile of v2, /device:TPU:1, one launch (start us, length us, event | category | flops | bytes accessed | tf_op | source)
XLA Modules:
  0.0 53.7 jit_solution(9264599502599314328)
XLA Ops:
  0.0 2.3 %to_modes_chunks.1 = (f32[16,64,128]{2,1,0:T(8,128)}, s32[24,256]{1,0:T(8,128)S(1)}) custom-call(f32[128,512]{1,0:T(8,128)} %rhs_hbm.1, f32[128,128]{1,0:T(8,128)} %modes_hbm.1, f32[1,128]{1,0:T(1,128)} %bitcast.5, s32[8,256]{1,0:T(8,128)} %ids_hbm.1, s32[8,256]{1,0:T(8,128)} %orientation_hbm.1, s32[1,256]{1,0:T(1,128)} %bitcast.4), custom_call_target="tpu_custom_call" | custom-call | flops 83886080 | bytes 1048576 | tf_op jit(solution)/shard_map/to_modes_chunks/pallas_call | solution.py:275
  2.3 10.2 %all-to-all-start = ((f32[16,64,128]{2,1,0:T(8,128)}), f32[16,64,128]{2,1,0:T(8,128)S(1)}, u32[]{:S(2)}, u32[]{:S(2)}) async-start(f32[16,64,128]{2,1,0:T(8,128)} %get-tuple-element.14), calls=%async_computation | async-start | bytes 1048576 | tf_op jit(solution)/shard_map/all_to_all | solution.py:291
  12.6 3.3 %collective-permute-start = (s32[24,256]{1,0:T(8,128)S(1)}, s32[24,256]{1,0:T(8,128)S(1)}, u32[]{:S(2)}, u32[]{:S(2)}) collective-permute-start(s32[24,256]{1,0:T(8,128)S(1)} %get-tuple-element.15.own_ref), channel_id=1, source_target_pairs={{0,8},{8,0},{16,24},{24,16},{32,40},{40,32},{48,56},{56,48},{64,72... | collective-permute-start | bytes 73736 | tf_op jit(solution)/shard_map/ppermute | solution.py:292
  15.9 0.1 pad_add_fusion.place_ref
  16.0 1.6 %own_tables.1 = (bf16[4,6,128,256]{3,2,1,0:T(8,128)(2,1)S(1)}, s32[2,8,128]{2,1,0:T(8,128)S(1)}, f32[16,128]{1,0:T(8,128)S(1)}, f32[2,8,128]{2,1,0:T(8,128)S(1)}...) custom-call(s32[2]{0:T(128)S(1)} %pad_add_fusion.place_ref, ...), custom_call_target="tpu_custom_call" | custom-call | flops 268435456 | bytes 2097152 | tf_op jit(solution)/shard_map/own_tables/pallas_call | solution.py:293
  17.6 8.9 %collective-permute-start.1 = (s32[24,256]{1,0:T(8,128)S(1)}, s32[24,256]{1,0:T(8,128)S(1)}, u32[]{:S(2)}, u32[]{:S(2)}) collective-permute-start(s32[24,256]{1,0:T(8,128)S(1)} %get-tuple-element.16), channel_id=1, source_target_pairs={{0,504},{8,16},{16,8},{24,32},{32,24},{40,48},{48,40},{56,64},{64,... | collective-permute-start | bytes 73736 | tf_op jit(solution)/shard_map/ppermute | solution.py:315
  26.6 0.0 collective-permute-done.source_table_ref
  26.6 1.2 %collective-permute-done.1.target_table_ref = s32[24,256]{1,0:T(8,128)S(1)} collective-permute-done((s32[24,256]{1,0:T(8,128)S(1)}, s32[24,256]{1,0:T(8,128)S(1)}, u32[]{:S(2)}, u32[]{:S(2)}) %collective-permute-start.1) | collective-permute-done | bytes 24608 | tf_op jit(solution)/shard_map/ppermute | solution.py:315
  27.8 0.0 all-to-all-done.x_ref
  27.8 0.0 copy-start
  27.8 4.8 %two_sweeps.1 = f32[16,64,128]{2,1,0:T(8,128)S(1)} custom-call(s32[2]{0:T(128)S(1)} %pad_add_fusion.place_ref, f32[16,64,128]{2,1,0:T(8,128)S(1)} %all-to-all-done.x_ref, s32[24,256]{1,0:T(8,128)S(1)} %collective-permute-done.source_table_ref, s32[24,256]{1,0:T(8,128)S(1)} %collective-permute-done.1.target_table_ref, ...), custom_call_target="tpu_custom_call" | custom-call | flops 4294967296 | bytes 8388608 | tf_op jit(solution)/shard_map/two_sweeps/pallas_call | solution.py:316
  32.6 19.9 %all_to_all.10.parts_ref = f32[16,64,128]{2,1,0:T(8,128)S(1)} all-to-all(f32[16,64,128]{2,1,0:T(8,128)S(1)} %two_sweeps.1), channel_id=1, replica_groups={{504,505,506,507,508,509,510,511,0,1,2,3,4,5,6,7},{8,9,10,11,12,13,14,1..., dimensions={0} | all-to-all | bytes 1048576 | tf_op jit(solution)/shard_map/all_to_all | solution.py:333
  52.4 0.0 copy-done
  52.4 1.3 %to_levels.1 = f32[128,512]{1,0:T(8,128)} custom-call(f32[16,64,128]{2,1,0:T(8,128)S(1)} %all_to_all.10.parts_ref, f32[128,128]{1,0:T(8,128)S(1)} %copy-done), custom_call_target="tpu_custom_call" | custom-call | flops 83886080 | bytes 1048576 | tf_op jit(solution)/shard_map/to_levels/pallas_call | solution.py:334
Async XLA Ops:
  2.3 25.4 %all-to-all-start = ((f32[16,64,128]{2,1,0:T(8,128)}), f32[16,64,128]{2,1,0:T(8,128)S(1)}, u32[]{:S(2)}, u32[]{:S(2)}) async-start(f32[16,64,128]{2,1,0:T(8,128)} %get-tuple-element.14), calls=%async_computation | async-start | bytes 1048576 | tf_op jit(solution)/shard_map/all_to_all | solution.py:291
  12.6 14.0 %collective-permute-start = (s32[24,256]{1,0:T(8,128)S(1)}, s32[24,256]{1,0:T(8,128)S(1)}, u32[]{:S(2)}, u32[]{:S(2)}) collective-permute-start(s32[24,256]{1,0:T(8,128)S(1)} %get-tuple-element.15.own_ref), channel_id=1, source_target_pairs={{0,8},{8,0},{16,24},{24,16},{32,40},{40,32},{48,56},{56,48},{64,72... | collective-permute-start | bytes 73736 | tf_op jit(solution)/shard_map/ppermute | solution.py:292
  17.6 10.2 %collective-permute-start.1 = (s32[24,256]{1,0:T(8,128)S(1)}, s32[24,256]{1,0:T(8,128)S(1)}, u32[]{:S(2)}, u32[]{:S(2)}) collective-permute-start(s32[24,256]{1,0:T(8,128)S(1)} %get-tuple-element.16), channel_id=1, source_target_pairs={{0,504},{8,16},{16,8},{24,32},{32,24},{40,48},{48,40},{56,64},{64,... | collective-permute-start | bytes 73736 | tf_op jit(solution)/shard_map/ppermute | solution.py:315
  27.8 24.7 %copy-start = (f32[128,128]{1,0:T(8,128)S(1)}, f32[128,128]{1,0:T(8,128)}, u32[]{:S(2)}) copy-start(f32[128,128]{1,0:T(8,128)} %levels_ref.1) | copy-start | bytes 196612

commit v3 on v2

--- a/solution.py
+++ b/solution.py
@@ -112,9 +112,8 @@
 
 def tables_kernel(
     place_ref, own_ref, helmholtz_hbm, inverse_hbm,
-    pick_ref, code_ref, weight_ref, inv_ref, high_ref, low_ref, again_ref, helmholtz_ref, inverse_ref, sems,
+    pick_ref, code_ref, weight_ref, inv_ref, high_ref, low_ref, helmholtz_ref, inverse_ref, sems,
 ):
-    again_ref[...] = own_ref[...]
     copies = fetch(((helmholtz_hbm, helmholtz_ref), (inverse_hbm, inverse_ref)), sems)
     odd = place_ref[0] == 1
     for half in (0, 1):
@@ -263,14 +262,14 @@
 def body(blocks, levels_rhs, to_modes, from_modes, helmholtz, local_inverse, neighbor_ids, neighbor_count, orientation):
     axes = ("elem", "mode")
     parts = lax.axis_size("mode")
-    source_pairs = [[(2 * k + i) * parts + j for i in range(2) for j in range(parts)] for k in range(blocks // 2)]
-    target_pairs = [
+    source_pairs = [
         [((2 * k - 1 + i) % blocks) * parts + j for i in range(2) for j in range(parts)] for k in range(blocks // 2)
     ]
-    source_swap = [(b, b ^ 1) for b in range(blocks)]
-    target_swap = [(b, (((b + 1) ^ 1) - 1) % blocks) for b in range(blocks)]
+    target_pairs = [[(2 * k + i) * parts + j for i in range(2) for j in range(parts)] for k in range(blocks // 2)]
+    source_swap = [(b, (((b + 1) ^ 1) - 1) % blocks) for b in range(blocks)]
+    target_swap = [(b, b ^ 1) for b in range(blocks)]
     helmholtz = helmholtz[None]
-    place = jnp.stack([lax.axis_index("elem") % 2, lax.axis_index("mode")]).astype(jnp.int32)
+    place = jnp.stack([(lax.axis_index("elem") + 1) % 2, lax.axis_index("mode")]).astype(jnp.int32)
 
     start, own = pl.pallas_call(
         to_modes_kernel,
@@ -289,8 +288,9 @@
         name="to_modes_chunks",
     )(*[far(x) for x in (levels_rhs, to_modes, helmholtz, neighbor_ids, orientation, neighbor_count[None])])
     sources = lax.all_to_all(start, axes, 0, 0, axis_index_groups=source_pairs, tiled=True)
+    target_table = lax.ppermute(own, "elem", target_swap)
     source_table = lax.ppermute(own, "elem", source_swap)
-    *parts_of_tables, again = pl.pallas_call(
+    parts_of_tables = pl.pallas_call(
         tables_kernel,
         out_shape=(
             pltpu.VMEM((4, 6, 128, 256), jnp.bfloat16),
@@ -299,10 +299,9 @@
             pltpu.VMEM((2, 8, 128), jnp.float32),
             pltpu.VMEM((256, 256), jnp.bfloat16),
             pltpu.VMEM((256, 256), jnp.bfloat16),
-            pltpu.VMEM((24, 256), jnp.int32),
         ),
         in_specs=[SMEM, VMEM, HBM, HBM],
-        out_specs=(VMEM,) * 7,
+        out_specs=(VMEM,) * 6,
         scratch_shapes=[
             pltpu.VMEM((1, 128), jnp.float32),
             pltpu.VMEM((16, 16), jnp.float32),
@@ -312,7 +311,6 @@
         cost_estimate=cost(1 << 28, 2 << 20),
         name="own_tables",
     )(place, near(own), far(helmholtz), far(local_inverse))
-    target_table = lax.ppermute(again, "elem", target_swap)
     targets = pl.pallas_call(
         sweep_kernel,
         out_shape=pltpu.VMEM((16, 64, 128), jnp.float32),

time: 54 us -> 51.3 us (0.950)
  blocking collectives: 19.9 us -> 15.4 us
  starting transfers between devices: 22.5 us -> 23.5 us
  waiting for transfers between devices: 1.2 us -> 2.03 us
    all_to_all x1, starting transfers between devices: 10.2 us -> 17.4 us  [body(): lax.all_to_all(start, axes, 0, 0, axis_index_groups=source_pairs, tiled=T...]
    ppermute x1, starting transfers between devices: 8.95 us -> 1.91 us  [body(): target_table = lax.ppermute(own, 'elem', target_swap)]
    all_to_all x1, blocking collectives: 19.9 us -> 15.4 us  [body(): lax.all_to_all(targets, axes, 0, 0, axis_index_groups=target_pairs, tiled...]
    ppermute x1, waiting for transfers between devices: 0.01 us -> 2.03 us  [body(): source_table = lax.ppermute(own, 'elem', source_swap)]
    ppermute x1, waiting for transfers between devices: 1.19 us -> 0.01 us  [body(): target_table = lax.ppermute(own, 'elem', target_swap)]
    ppermute x1, starting transfers between devices: 3.33 us -> 4.15 us  [body(): source_table = lax.ppermute(own, 'elem', source_swap)]
where the time goes in v3:
time: 51.3 us; the launch traced here: 51 us
  starting transfers between devices  23.5 us (46%)
  blocking collectives  15.4 us (30%)
  Pallas kernels  9.99 us (19%)
  waiting for transfers between devices  2.03 us (4%)
    all_to_all x1, starting transfers between devices, body(): lax.all_to_all(start, axes, 0, 0, axis_index_groups=source_pairs, tiled=T...  17.4 us
    all_to_all x1, blocking collectives, body(): lax.all_to_all(targets, axes, 0, 0, axis_index_groups=target_pairs, tiled...  15.4 us
    pallas_call x1, Pallas kernels, body(): pl.pallas_call(sweep_kernel, out_shape=pltpu.VMEM((16, 64, 128), jnp.floa...  4.79 us
    ppermute x1, starting transfers between devices, body(): source_table = lax.ppermute(own, 'elem', source_swap)  4.15 us
    pallas_call x1, Pallas kernels, body(): pl.pallas_call(to_modes_kernel, out_shape=(pltpu.VMEM((16, 64, 128), jnp....  2.34 us
    ppermute x1, waiting for transfers between devices, body(): source_table = lax.ppermute(own, 'elem', source_swap)  2.03 us
    ppermute x1, starting transfers between devices, body(): target_table = lax.ppermute(own, 'elem', target_swap)  1.91 us
    pallas_call x1, Pallas kernels, body(): pl.pallas_call(tables_kernel, out_shape=(pltpu.VMEM((4, 6, 128, 256), jnp...  1.6 us
  transfers between devices with their start and end apart: 3, of which 1 were waited for; matrix products, arithmetic and copies ran while one was open for 0% of the time, Pallas kernels for 3%

profile of v3, /device:TPU:1, one launch (start us, length us, event | category | flops | bytes accessed | tf_op | source)
XLA Modules:
  0.0 51.0 jit_solution(8556177894488317120)
XLA Ops:
  0.0 2.3 %to_modes_chunks.1 = (f32[16,64,128]{2,1,0:T(8,128)}, s32[24,256]{1,0:T(8,128)S(1)}) custom-call(f32[128,512]{1,0:T(8,128)} %rhs_hbm.1, f32[128,128]{1,0:T(8,128)} %modes_hbm.1, f32[1,128]{1,0:T(1,128)} %bitcast.5, s32[8,256]{1,0:T(8,128)} %ids_hbm.1, s32[8,256]{1,0:T(8,128)} %orientation_hbm.1, s32[1,256]{1,0:T(1,128)} %bitcast.4), custom_call_target="tpu_custom_call" | custom-call | flops 83886080 | bytes 1048576 | tf_op jit(solution)/shard_map/to_modes_chunks/pallas_call | solution.py:274
  2.3 17.4 %all-to-all-start = ((f32[16,64,128]{2,1,0:T(8,128)}), f32[16,64,128]{2,1,0:T(8,128)S(1)}, u32[]{:S(2)}, u32[]{:S(2)}) async-start(f32[16,64,128]{2,1,0:T(8,128)} %get-tuple-element.13), calls=%async_computation | async-start | bytes 1048576 | tf_op jit(solution)/shard_map/all_to_all | solution.py:290
  19.8 1.9 %collective-permute-start.1 = (s32[24,256]{1,0:T(8,128)S(1)}, s32[24,256]{1,0:T(8,128)S(1)}, u32[]{:S(2)}, u32[]{:S(2)}) collective-permute-start(s32[24,256]{1,0:T(8,128)S(1)} %get-tuple-element.14.own_ref), channel_id=1, source_target_pairs={{0,8},{8,0},{16,24},{24,16},{32,40},{40,32},{48,56},{56,48},{64,72... | collective-permute-start | bytes 73736 | tf_op jit(solution)/shard_map/ppermute | solution.py:291
  21.7 4.1 %collective-permute-start = (s32[24,256]{1,0:T(8,128)S(1)}, s32[24,256]{1,0:T(8,128)S(1)}, u32[]{:S(2)}, u32[]{:S(2)}) collective-permute-start(s32[24,256]{1,0:T(8,128)S(1)} %get-tuple-element.14.own_ref), channel_id=1, source_target_pairs={{0,504},{8,16},{16,8},{24,32},{32,24},{40,48},{48,40},{56,64},{64,... | collective-permute-start | bytes 73736 | tf_op jit(solution)/shard_map/ppermute | solution.py:292
  25.8 0.1 pad_add_fusion.place_ref
  25.9 1.6 %own_tables.1 = (bf16[4,6,128,256]{3,2,1,0:T(8,128)(2,1)S(1)}, s32[2,8,128]{2,1,0:T(8,128)S(1)}, f32[16,128]{1,0:T(8,128)S(1)}, f32[2,8,128]{2,1,0:T(8,128)S(1)}...) custom-call(s32[2]{0:T(128)S(1)} %pad_add_fusion.place_ref, s32[24,256]{1,0:T(8,128)S(1)} %get-tuple-element.14.own_ref, ...), custom_call_target="tpu_custom_call" | custom-call | flops 268435456 | bytes 2097152 | tf_op jit(solution)/shard_map/own_tables/pallas_call | solution.py:293
  27.5 0.0 collective-permute-done.1.target_table_ref
  27.5 2.0 %collective-permute-done.source_table_ref = s32[24,256]{1,0:T(8,128)S(1)} collective-permute-done((s32[24,256]{1,0:T(8,128)S(1)}, s32[24,256]{1,0:T(8,128)S(1)}, u32[]{:S(2)}, u32[]{:S(2)}) %collective-permute-start) | collective-permute-done | bytes 24608 | tf_op jit(solution)/shard_map/ppermute | solution.py:292
  29.6 0.0 all-to-all-done.x_ref
  29.6 0.0 copy-start
  29.6 4.8 %two_sweeps.1 = f32[16,64,128]{2,1,0:T(8,128)S(1)} custom-call(s32[2]{0:T(128)S(1)} %pad_add_fusion.place_ref, f32[16,64,128]{2,1,0:T(8,128)S(1)} %all-to-all-done.x_ref, s32[24,256]{1,0:T(8,128)S(1)} %collective-permute-done.source_table_ref, s32[24,256]{1,0:T(8,128)S(1)} %collective-permute-done.1.target_table_ref, ...), custom_call_target="tpu_custom_call" | custom-call | flops 4294967296 | bytes 8388608 | tf_op jit(solution)/shard_map/two_sweeps/pallas_call | solution.py:314
  34.4 15.4 %all_to_all.10.parts_ref = f32[16,64,128]{2,1,0:T(8,128)S(1)} all-to-all(f32[16,64,128]{2,1,0:T(8,128)S(1)} %two_sweeps.1), channel_id=1, replica_groups={{0,1,2,3,4,5,6,7,8,9,10,11,12,13,14,15},{16,17,18,19,20,21,22,23,24,25,..., dimensions={0} | all-to-all | bytes 1048576 | tf_op jit(solution)/shard_map/all_to_all | solution.py:331
  49.7 0.0 copy-done
  49.7 1.3 %to_levels.1 = f32[128,512]{1,0:T(8,128)} custom-call(f32[16,64,128]{2,1,0:T(8,128)S(1)} %all_to_all.10.parts_ref, f32[128,128]{1,0:T(8,128)S(1)} %copy-done), custom_call_target="tpu_custom_call" | custom-call | flops 83886080 | bytes 1048576 | tf_op jit(solution)/shard_map/to_levels/pallas_call | solution.py:332
Async XLA Ops:
  2.3 27.2 %all-to-all-start = ((f32[16,64,128]{2,1,0:T(8,128)}), f32[16,64,128]{2,1,0:T(8,128)S(1)}, u32[]{:S(2)}, u32[]{:S(2)}) async-start(f32[16,64,128]{2,1,0:T(8,128)} %get-tuple-element.13), calls=%async_computation | async-start | bytes 1048576 | tf_op jit(solution)/shard_map/all_to_all | solution.py:290
  19.8 7.8 %collective-permute-start.1 = (s32[24,256]{1,0:T(8,128)S(1)}, s32[24,256]{1,0:T(8,128)S(1)}, u32[]{:S(2)}, u32[]{:S(2)}) collective-permute-start(s32[24,256]{1,0:T(8,128)S(1)} %get-tuple-element.14.own_ref), channel_id=1, source_target_pairs={{0,8},{8,0},{16,24},{24,16},{32,40},{40,32},{48,56},{56,48},{64,72... | collective-permute-start | bytes 73736 | tf_op jit(solution)/shard_map/ppermute | solution.py:291
  21.7 7.9 %collective-permute-start = (s32[24,256]{1,0:T(8,128)S(1)}, s32[24,256]{1,0:T(8,128)S(1)}, u32[]{:S(2)}, u32[]{:S(2)}) collective-permute-start(s32[24,256]{1,0:T(8,128)S(1)} %get-tuple-element.14.own_ref), channel_id=1, source_target_pairs={{0,504},{8,16},{16,8},{24,32},{32,24},{40,48},{48,40},{56,64},{64,... | collective-permute-start | bytes 73736 | tf_op jit(solution)/shard_map/ppermute | solution.py:292
  29.6 20.2 %copy-start = (f32[128,128]{1,0:T(8,128)S(1)}, f32[128,128]{1,0:T(8,128)}, u32[]{:S(2)}) copy-start(f32[128,128]{1,0:T(8,128)} %levels_ref.1) | copy-start | bytes 196612

commit v4 on v3

--- a/solution.py
+++ b/solution.py
@@ -163,7 +163,7 @@
 
 
 def sweep_kernel(
-    place_ref, x_ref, source_table_ref, target_table_ref, pick_ref, code_ref, weight_ref, inv_ref, high_ref, low_ref,
+    place_ref, x_ref, target_table_ref, source_table_ref, pick_ref, code_ref, weight_ref, inv_ref, high_ref, low_ref,
     out_ref, u_ref, w_ref, us_ref, ws_ref, s_ref, other_ref,
 ):
     odd = place_ref[0] == 1
@@ -288,8 +288,8 @@
         name="to_modes_chunks",
     )(*[far(x) for x in (levels_rhs, to_modes, helmholtz, neighbor_ids, orientation, neighbor_count[None])])
     sources = lax.all_to_all(start, axes, 0, 0, axis_index_groups=source_pairs, tiled=True)
+    source_table = lax.ppermute(own, "elem", source_swap)
     target_table = lax.ppermute(own, "elem", target_swap)
-    source_table = lax.ppermute(own, "elem", source_swap)
     parts_of_tables = pl.pallas_call(
         tables_kernel,
         out_shape=(
@@ -327,7 +327,7 @@
         compiler_params=LIMIT,
         cost_estimate=cost(4 << 30, 8 << 20),
         name="two_sweeps",
-    )(place, near(sources), near(source_table), near(target_table), *[near(part) for part in parts_of_tables])
+    )(place, near(sources), near(target_table), near(source_table), *[near(part) for part in parts_of_tables])
     whole = lax.all_to_all(targets, axes, 0, 0, axis_index_groups=target_pairs, tiled=True)
     return pl.pallas_call(
         to_levels_kernel,

time: 51.3 us -> 49.4 us (0.963)
  starting transfers between devices: 23.5 us -> 21.3 us
  waiting for transfers between devices: 2.03 us -> 3.52 us
  blocking collectives: 15.4 us -> 14.1 us
    ppermute x1, starting transfers between devices: 4.15 us -> 2 us  [body(): source_table = lax.ppermute(own, 'elem', source_swap)]
    all_to_all x1, blocking collectives: 15.4 us -> 14.1 us  [body(): lax.all_to_all(targets, axes, 0, 0, axis_index_groups=target_pairs, tiled...]
    all_to_all x1, waiting for transfers between devices: 0.01 us -> 1.28 us  [body(): lax.all_to_all(start, axes, 0, 0, axis_index_groups=source_pairs, tiled=T...]
  transfers between devices with their start and end apart: 3 -> 3, of which waited for: 1 -> 2; matrix products, arithmetic and copies ran while one was open for 0% -> 0% of each run, Pallas kernels for 3% -> 3%
where the time goes in v4:
time: 49.4 us; the launch traced here: 49.1 us
  starting transfers between devices  21.3 us (43%)
  blocking collectives  14.1 us (29%)
  Pallas kernels  10 us (20%)
  waiting for transfers between devices  3.52 us (7%)
    all_to_all x1, starting transfers between devices, body(): lax.all_to_all(start, axes, 0, 0, axis_index_groups=source_pairs, tiled=T...  17.4 us
    all_to_all x1, blocking collectives, body(): lax.all_to_all(targets, axes, 0, 0, axis_index_groups=target_pairs, tiled...  14.1 us
    pallas_call x1, Pallas kernels, body(): pl.pallas_call(sweep_kernel, out_shape=pltpu.VMEM((16, 64, 128), jnp.floa...  4.8 us
    pallas_call x1, Pallas kernels, body(): pl.pallas_call(to_modes_kernel, out_shape=(pltpu.VMEM((16, 64, 128), jnp....  2.34 us
    ppermute x1, waiting for transfers between devices, body(): source_table = lax.ppermute(own, 'elem', source_swap)  2.24 us
    ppermute x1, starting transfers between devices, body(): source_table = lax.ppermute(own, 'elem', source_swap)  2 us
    ppermute x1, starting transfers between devices, body(): target_table = lax.ppermute(own, 'elem', target_swap)  1.92 us
    pallas_call x1, Pallas kernels, body(): pl.pallas_call(tables_kernel, out_shape=(pltpu.VMEM((4, 6, 128, 256), jnp...  1.6 us
  transfers between devices with their start and end apart: 3, of which 2 were waited for; matrix products, arithmetic and copies ran while one was open for 0% of the time, Pallas kernels for 3%

profile of v4, /device:TPU:1, one launch (start us, length us, event | category | flops | bytes accessed | tf_op | source)
XLA Modules:
  0.0 49.1 jit_solution(9279043943066308140)
XLA Ops:
  0.0 2.3 %to_modes_chunks.1 = (f32[16,64,128]{2,1,0:T(8,128)}, s32[24,256]{1,0:T(8,128)S(1)}) custom-call(f32[128,512]{1,0:T(8,128)} %rhs_hbm.1, f32[128,128]{1,0:T(8,128)} %modes_hbm.1, f32[1,128]{1,0:T(1,128)} %bitcast.5, s32[8,256]{1,0:T(8,128)} %ids_hbm.1, s32[8,256]{1,0:T(8,128)} %orientation_hbm.1, s32[1,256]{1,0:T(1,128)} %bitcast.4), custom_call_target="tpu_custom_call" | custom-call | flops 83886080 | bytes 1048576 | tf_op jit(solution)/shard_map/to_modes_chunks/pallas_call | solution.py:274
  2.3 17.4 %all-to-all-start = ((f32[16,64,128]{2,1,0:T(8,128)}), f32[16,64,128]{2,1,0:T(8,128)S(1)}, u32[]{:S(2)}, u32[]{:S(2)}) async-start(f32[16,64,128]{2,1,0:T(8,128)} %get-tuple-element.13), calls=%async_computation | async-start | bytes 1048576 | tf_op jit(solution)/shard_map/all_to_all | solution.py:290
  19.8 2.0 %collective-permute-start.1 = (s32[24,256]{1,0:T(8,128)S(1)}, s32[24,256]{1,0:T(8,128)S(1)}, u32[]{:S(2)}, u32[]{:S(2)}) collective-permute-start(s32[24,256]{1,0:T(8,128)S(1)} %get-tuple-element.14.own_ref), channel_id=1, source_target_pairs={{0,504},{8,16},{16,8},{24,32},{32,24},{40,48},{48,40},{56,64},{64,... | collective-permute-start | bytes 73736 | tf_op jit(solution)/shard_map/ppermute | solution.py:291
  21.8 1.9 %collective-permute-start = (s32[24,256]{1,0:T(8,128)S(1)}, s32[24,256]{1,0:T(8,128)S(1)}, u32[]{:S(2)}, u32[]{:S(2)}) collective-permute-start(s32[24,256]{1,0:T(8,128)S(1)} %get-tuple-element.14.own_ref), channel_id=1, source_target_pairs={{0,8},{8,0},{16,24},{24,16},{32,40},{40,32},{48,56},{56,48},{64,72... | collective-permute-start | bytes 73736 | tf_op jit(solution)/shard_map/ppermute | solution.py:292
  23.7 0.1 pad_add_fusion.place_ref
  23.8 1.6 %own_tables.1 = (bf16[4,6,128,256]{3,2,1,0:T(8,128)(2,1)S(1)}, s32[2,8,128]{2,1,0:T(8,128)S(1)}, f32[16,128]{1,0:T(8,128)S(1)}, f32[2,8,128]{2,1,0:T(8,128)S(1)}...) custom-call(s32[2]{0:T(128)S(1)} %pad_add_fusion.place_ref, s32[24,256]{1,0:T(8,128)S(1)} %get-tuple-element.14.own_ref, ...), custom_call_target="tpu_custom_call" | custom-call | flops 268435456 | bytes 2097152 | tf_op jit(solution)/shard_map/own_tables/pallas_call | solution.py:293
  25.4 2.2 %collective-permute-done.1.source_table_ref = s32[24,256]{1,0:T(8,128)S(1)} collective-permute-done((s32[24,256]{1,0:T(8,128)S(1)}, s32[24,256]{1,0:T(8,128)S(1)}, u32[]{:S(2)}, u32[]{:S(2)}) %collective-permute-start.1) | collective-permute-done | bytes 24608 | tf_op jit(solution)/shard_map/ppermute | solution.py:291
  27.6 0.0 collective-permute-done.target_table_ref
  27.6 1.3 %all-to-all-done.x_ref = f32[16,64,128]{2,1,0:T(8,128)S(1)} async-done(((f32[16,64,128]{2,1,0:T(8,128)}), f32[16,64,128]{2,1,0:T(8,128)S(1)}, u32[]{:S(2)}, u32[]{:S(2)}) %all-to-all-start) | async-done | bytes 524320 | tf_op jit(solution)/shard_map/all_to_all | solution.py:290
  28.9 0.0 copy-start
  28.9 4.8 %two_sweeps.1 = f32[16,64,128]{2,1,0:T(8,128)S(1)} custom-call(s32[2]{0:T(128)S(1)} %pad_add_fusion.place_ref, f32[16,64,128]{2,1,0:T(8,128)S(1)} %all-to-all-done.x_ref, s32[24,256]{1,0:T(8,128)S(1)} %collective-permute-done.target_table_ref, s32[24,256]{1,0:T(8,128)S(1)} %collective-permute-done.1.source_table_ref, ...), custom_call_target="tpu_custom_call" | custom-call | flops 4294967296 | bytes 8388608 | tf_op jit(solution)/shard_map/two_sweeps/pallas_call | solution.py:314
  33.7 14.1 %all_to_all.10.parts_ref = f32[16,64,128]{2,1,0:T(8,128)S(1)} all-to-all(f32[16,64,128]{2,1,0:T(8,128)S(1)} %two_sweeps.1), channel_id=1, replica_groups={{0,1,2,3,4,5,6,7,8,9,10,11,12,13,14,15},{16,17,18,19,20,21,22,23,24,25,..., dimensions={0} | all-to-all | bytes 1048576 | tf_op jit(solution)/shard_map/all_to_all | solution.py:331
  47.8 0.0 copy-done
  47.8 1.3 %to_levels.1 = f32[128,512]{1,0:T(8,128)} custom-call(f32[16,64,128]{2,1,0:T(8,128)S(1)} %all_to_all.10.parts_ref, f32[128,128]{1,0:T(8,128)S(1)} %copy-done), custom_call_target="tpu_custom_call" | custom-call | flops 83886080 | bytes 1048576 | tf_op jit(solution)/shard_map/to_levels/pallas_call | solution.py:332
Async XLA Ops:
  2.3 26.6 %all-to-all-start = ((f32[16,64,128]{2,1,0:T(8,128)}), f32[16,64,128]{2,1,0:T(8,128)S(1)}, u32[]{:S(2)}, u32[]{:S(2)}) async-start(f32[16,64,128]{2,1,0:T(8,128)} %get-tuple-element.13), calls=%async_computation | async-start | bytes 1048576 | tf_op jit(solution)/shard_map/all_to_all | solution.py:290
  19.8 7.9 %collective-permute-start.1 = (s32[24,256]{1,0:T(8,128)S(1)}, s32[24,256]{1,0:T(8,128)S(1)}, u32[]{:S(2)}, u32[]{:S(2)}) collective-permute-start(s32[24,256]{1,0:T(8,128)S(1)} %get-tuple-element.14.own_ref), channel_id=1, source_target_pairs={{0,504},{8,16},{16,8},{24,32},{32,24},{40,48},{48,40},{56,64},{64,... | collective-permute-start | bytes 73736 | tf_op jit(solution)/shard_map/ppermute | solution.py:291
  21.8 5.9 %collective-permute-start = (s32[24,256]{1,0:T(8,128)S(1)}, s32[24,256]{1,0:T(8,128)S(1)}, u32[]{:S(2)}, u32[]{:S(2)}) collective-permute-start(s32[24,256]{1,0:T(8,128)S(1)} %get-tuple-element.14.own_ref), channel_id=1, source_target_pairs={{0,8},{8,0},{16,24},{24,16},{32,40},{40,32},{48,56},{56,48},{64,72... | collective-permute-start | bytes 73736 | tf_op jit(solution)/shard_map/ppermute | solution.py:292
  28.9 18.9 %copy-start = (f32[128,128]{1,0:T(8,128)S(1)}, f32[128,128]{1,0:T(8,128)}, u32[]{:S(2)}) copy-start(f32[128,128]{1,0:T(8,128)} %levels_ref.1) | copy-start | bytes 196612

commit v5 on v4

--- a/solution.py
+++ b/solution.py
@@ -21,6 +21,34 @@
     ah, al = split(a)
     bh, bl = split(b)
     return dot(ah, bh) + (dot(ah, bl) + dot(al, bh))
+
+
+def point_keys(index, spread):
+    if spread:
+        e, p = index >> 4, index & 15
+        i, j = p >> 2, p & 3
+        high_i, high_j = i >> 1, j >> 1
+        a = jnp.where(high_i == 1, 3 - i, i)
+        b = jnp.where(high_j == 1, 3 - j, j)
+        return e * 4 + a * 2 + b, high_i * 2 + high_j
+    t, e = index >> 5, index & 31
+    return e * 4 + (t & 3), t >> 2
+
+
+def parity_matrix(t, p, scale):
+    i, j = p >> 2, p & 3
+    near = jnp.where(i > 1, 3 - i, i) * 2 + jnp.where(j > 1, 3 - j, j)
+    odd = ((i >> 1) * 2 + (j >> 1)) & (t >> 2)
+    value = jnp.where((odd == 1) | (odd == 2), -scale, scale)
+    return jnp.where(near == (t & 3), value, 0.0).astype(jnp.bfloat16)
+
+
+def point_matrix(row_points, scale):
+    row, row_bits = point_keys(lax.broadcasted_iota(jnp.int32, (512, 1), 0), row_points)
+    col, col_bits = point_keys(lax.broadcasted_iota(jnp.int32, (1, 512), 1), not row_points)
+    odd = row_bits & col_bits
+    value = jnp.where((odd == 1) | (odd == 2), -scale, scale)
+    return jnp.where(row == col, value, 0.0).astype(jnp.bfloat16)
 
 
 def column(row):
@@ -51,15 +79,12 @@
         ),
         sems,
     )
-    row = lax.broadcasted_iota(jnp.int32, (512, 512), 0)
-    col = lax.broadcasted_iota(jnp.int32, (1, 512), 1)
-    perm = (row == (col % 32) * 16 + col // 32).astype(jnp.float32).astype(jnp.bfloat16)
+    points = point_matrix(True, 1.0)
     for copy in copies:
         copy.wait()
     table_ref[16:24] = jnp.broadcast_to(count_ref[...], (8, 256))
     high, low = split(rhs_ref[...])
-    high = dot(high, perm).astype(jnp.bfloat16)
-    low = dot(low, perm).astype(jnp.bfloat16)
+    high, low = split(dot(high, points) + dot(low, points))
     mh, ml = split(modes_ref[...] * column(1.0 / (1.0 + helmholtz_ref[...])))
     start = dot(mh, high) + (dot(mh, low) + dot(ml, high))
     for group in range(8):
@@ -112,7 +137,7 @@
 
 def tables_kernel(
     place_ref, own_ref, helmholtz_hbm, inverse_hbm,
-    pick_ref, code_ref, weight_ref, inv_ref, high_ref, low_ref, helmholtz_ref, inverse_ref, sems,
+    pick_ref, code_ref, weight_ref, inv_ref, high_ref, low_ref, back_ref, helmholtz_ref, inverse_ref, sems,
 ):
     copies = fetch(((helmholtz_hbm, helmholtz_ref), (inverse_hbm, inverse_ref)), sems)
     odd = place_ref[0] == 1
@@ -122,6 +147,7 @@
         inv_ref[half] = jnp.broadcast_to(inv, (8, 128))
     for copy in copies:
         copy.wait()
+    back_ref[...] = point_matrix(False, 0.25)
     rows = lax.broadcasted_iota(jnp.int32, (16, 128), 0)
     lanes = lax.broadcasted_iota(jnp.int32, (16, 128), 1)
     coeff = jnp.sum(jnp.where(lanes == rows + 16 * place_ref[1], helmholtz_ref[...], 0.0), axis=1, keepdims=True)
@@ -133,7 +159,13 @@
     same = (
         lax.broadcasted_iota(jnp.int32, (256, 256), 0) % 16 == lax.broadcasted_iota(jnp.int32, (256, 256), 1) % 16
     )
-    for ref, part in zip((high_ref, low_ref), split(inverse_ref[...])):
+    t = lax.broadcasted_iota(jnp.int32, (16, 16), 0)
+    p = lax.broadcasted_iota(jnp.int32, (16, 16), 1)
+    there = parity_matrix(t, p, 1.0)
+    high, low = split(inverse_ref[...])
+    high, low = split(dot(there, high) + dot(there, low))
+    again = parity_matrix(p, t, 0.25)
+    for ref, part in zip((high_ref, low_ref), split(dot(high, again) + dot(low, again))):
         ref[...] = jnp.where(same, dot(dot(rise, part).astype(jnp.bfloat16), spread), 0.0).astype(jnp.bfloat16)
 
 
@@ -146,13 +178,22 @@
         for side in range(2):
             code_k = jnp.broadcast_to(code[2 * pair + side : 2 * pair + side + 1], (8, 128))
             swap = (code_k & 1) == 1
-            flip_row = (code_k & 2) == 2
-            flip_col = (code_k & 4) == 4
+            by_row = jnp.where((code_k & 2) == 2, -1.0, 1.0)
+            by_col = jnp.where((code_k & 4) == 4, -1.0, 1.0)
+            by_both = by_row * by_col
             for m in range(2):
                 x = [found[16 * p + 8 * m : 16 * p + 8 * m + 8, 128 * side : 128 * side + 128] for p in range(16)]
-                x = [jnp.where(flip_row, x[4 * (3 - i) + j], x[4 * i + j]) for i in range(4) for j in range(4)]
-                x = [jnp.where(flip_col, x[4 * i + 3 - j], x[4 * i + j]) for i in range(4) for j in range(4)]
-                x = [x[5 * i] if i == j else jnp.where(swap, x[4 * j + i], x[4 * i + j]) for i in range(4) for j in range(4)]
+                even, col_odd, row_odd, odd = x[0:4], x[4:8], x[8:12], x[12:16]
+                col_odd = [v * by_col for v in col_odd]
+                row_odd = [v * by_row for v in row_odd]
+                odd = [v * by_both for v in odd]
+                turned = (0, 2, 1, 3)
+                x = (
+                    [even[i] if i == t else jnp.where(swap, even[t], even[i]) for i, t in enumerate(turned)]
+                    + [jnp.where(swap, row_odd[t], col_odd[i]) for i, t in enumerate(turned)]
+                    + [jnp.where(swap, col_odd[t], row_odd[i]) for i, t in enumerate(turned)]
+                    + [odd[i] if i == t else jnp.where(swap, odd[t], odd[i]) for i, t in enumerate(turned)]
+                )
                 total[m] = [v if t is None else t + v for t, v in zip(total[m], x)]
     return total
 
@@ -227,7 +268,7 @@
                 out_ref[base + j, 16 * quad : 16 * quad + 16, :] = part
 
 
-def to_levels_kernel(parts_ref, levels_ref, out_ref, modes_ref):
+def to_levels_kernel(parts_ref, levels_ref, back_ref, out_ref, modes_ref):
     for group in range(8):
         for quad in range(4):
             rows = slice(16 * quad, 16 * quad + 16)
@@ -235,10 +276,7 @@
                 parts_ref[group, rows, :] + parts_ref[8 + group, rows, :]
             )
     high, low = split(dot3(levels_ref[...], modes_ref[...]))
-    row = lax.broadcasted_iota(jnp.int32, (512, 512), 0)
-    col = lax.broadcasted_iota(jnp.int32, (1, 512), 1)
-    perm = (row == (col % 16) * 32 + col // 16).astype(jnp.float32).astype(jnp.bfloat16)
-    out_ref[...] = dot(high, perm) + dot(low, perm)
+    out_ref[...] = dot(high, back_ref[...]) + dot(low, back_ref[...])
 
 
 def cost(flops, moved):
@@ -290,7 +328,7 @@
     sources = lax.all_to_all(start, axes, 0, 0, axis_index_groups=source_pairs, tiled=True)
     source_table = lax.ppermute(own, "elem", source_swap)
     target_table = lax.ppermute(own, "elem", target_swap)
-    parts_of_tables = pl.pallas_call(
+    *parts_of_tables, back = pl.pallas_call(
         tables_kernel,
         out_shape=(
             pltpu.VMEM((4, 6, 128, 256), jnp.bfloat16),
@@ -299,9 +337,10 @@
             pltpu.VMEM((2, 8, 128), jnp.float32),
             pltpu.VMEM((256, 256), jnp.bfloat16),
             pltpu.VMEM((256, 256), jnp.bfloat16),
+            pltpu.VMEM((512, 512), jnp.bfloat16),
         ),
         in_specs=[SMEM, VMEM, HBM, HBM],
-        out_specs=(VMEM,) * 6,
+        out_specs=(VMEM,) * 7,
         scratch_shapes=[
             pltpu.VMEM((1, 128), jnp.float32),
             pltpu.VMEM((16, 16), jnp.float32),
@@ -332,13 +371,13 @@
     return pl.pallas_call(
         to_levels_kernel,
         out_shape=jax.ShapeDtypeStruct((128, 512), jnp.float32),
-        in_specs=[VMEM] * 2,
+        in_specs=[VMEM] * 3,
         out_specs=VMEM,
         scratch_shapes=[pltpu.VMEM((128, 512), jnp.float32)],
         compiler_params=LIMIT,
         cost_estimate=cost(2 * 128 * 512 * (512 + 128), 1 << 20),
         name="to_levels",
-    )(near(whole), from_modes)
+    )(near(whole), from_modes, near(back))
 
 
 def solution(mesh):

time: 49.4 us -> 49 us (level)
  waiting for transfers between devices: 3.52 us -> 2.95 us
    pallas_call x1, Pallas kernels: 1.6 us -> 2.17 us  [body(): pl.pallas_call(tables_kernel, out_shape=(pltpu.VMEM((4, 6, 128, 256), jnp...]
    ppermute x1, waiting for transfers between devices: 2.24 us -> 1.67 us  [body(): source_table = lax.ppermute(own, 'elem', source_swap)]
  transfers between devices with their start and end apart: 3 -> 3, of which waited for: 2 -> 2; matrix products, arithmetic and copies ran while one was open for 0% -> 0% of each run, Pallas kernels for 3% -> 4%
where the time goes in v5:
time: 49 us; the launch traced here: 48.6 us
  starting transfers between devices  21.3 us (43%)
  blocking collectives  14.1 us (29%)
  Pallas kernels  10.1 us (21%)
  waiting for transfers between devices  2.95 us (6%)
    all_to_all x1, starting transfers between devices, body(): lax.all_to_all(start, axes, 0, 0, axis_index_groups=source_pairs, tiled=T...  17.4 us
    all_to_all x1, blocking collectives, body(): lax.all_to_all(targets, axes, 0, 0, axis_index_groups=target_pairs, tiled...  14.1 us
    pallas_call x1, Pallas kernels, body(): pl.pallas_call(sweep_kernel, out_shape=pltpu.VMEM((16, 64, 128), jnp.floa...  4.33 us
    pallas_call x1, Pallas kernels, body(): pl.pallas_call(to_modes_kernel, out_shape=(pltpu.VMEM((16, 64, 128), jnp....  2.38 us
    pallas_call x1, Pallas kernels, body(): pl.pallas_call(tables_kernel, out_shape=(pltpu.VMEM((4, 6, 128, 256), jnp...  2.17 us
    ppermute x1, starting transfers between devices, body(): source_table = lax.ppermute(own, 'elem', source_swap)  2 us
    ppermute x1, starting transfers between devices, body(): target_table = lax.ppermute(own, 'elem', target_swap)  1.92 us
    ppermute x1, waiting for transfers between devices, body(): source_table = lax.ppermute(own, 'elem', source_swap)  1.67 us
  transfers between devices with their start and end apart: 3, of which 2 were waited for; matrix products, arithmetic and copies ran while one was open for 0% of the time, Pallas kernels for 4%

profile of v5, /device:TPU:1, one launch (start us, length us, event | category | flops | bytes accessed | tf_op | source)
XLA Modules:
  0.0 48.6 jit_solution(10278828758464495376)
XLA Ops:
  0.0 2.4 %to_modes_chunks.1 = (f32[16,64,128]{2,1,0:T(8,128)}, s32[24,256]{1,0:T(8,128)S(1)}) custom-call(f32[128,512]{1,0:T(8,128)} %rhs_hbm.1, f32[128,128]{1,0:T(8,128)} %modes_hbm.1, f32[1,128]{1,0:T(1,128)} %bitcast.5, s32[8,256]{1,0:T(8,128)} %ids_hbm.1, s32[8,256]{1,0:T(8,128)} %orientation_hbm.1, s32[1,256]{1,0:T(1,128)} %bitcast.4), custom_call_target="tpu_custom_call" | custom-call | flops 83886080 | bytes 1048576 | tf_op jit(solution)/shard_map/to_modes_chunks/pallas_call | solution.py:312
  2.4 17.4 %all-to-all-start = ((f32[16,64,128]{2,1,0:T(8,128)}), f32[16,64,128]{2,1,0:T(8,128)S(1)}, u32[]{:S(2)}, u32[]{:S(2)}) async-start(f32[16,64,128]{2,1,0:T(8,128)} %get-tuple-element.14), calls=%async_computation | async-start | bytes 1048576 | tf_op jit(solution)/shard_map/all_to_all | solution.py:328
  19.8 2.0 %collective-permute-start.1 = (s32[24,256]{1,0:T(8,128)S(1)}, s32[24,256]{1,0:T(8,128)S(1)}, u32[]{:S(2)}, u32[]{:S(2)}) collective-permute-start(s32[24,256]{1,0:T(8,128)S(1)} %get-tuple-element.15.own_ref), channel_id=1, source_target_pairs={{0,504},{8,16},{16,8},{24,32},{32,24},{40,48},{48,40},{56,64},{64,... | collective-permute-start | bytes 73736 | tf_op jit(solution)/shard_map/ppermute | solution.py:329
  21.8 1.9 %collective-permute-start = (s32[24,256]{1,0:T(8,128)S(1)}, s32[24,256]{1,0:T(8,128)S(1)}, u32[]{:S(2)}, u32[]{:S(2)}) collective-permute-start(s32[24,256]{1,0:T(8,128)S(1)} %get-tuple-element.15.own_ref), channel_id=1, source_target_pairs={{0,8},{8,0},{16,24},{24,16},{32,40},{40,32},{48,56},{56,48},{64,72... | collective-permute-start | bytes 73736 | tf_op jit(solution)/shard_map/ppermute | solution.py:330
  23.8 0.1 pad_add_fusion.place_ref
  23.8 2.2 %own_tables.1 = (bf16[4,6,128,256]{3,2,1,0:T(8,128)(2,1)S(1)}, s32[2,8,128]{2,1,0:T(8,128)S(1)}, f32[16,128]{1,0:T(8,128)S(1)}, f32[2,8,128]{2,1,0:T(8,128)S(1)}...) custom-call(s32[2]{0:T(128)S(1)} %pad_add_fusion.place_ref, ...), custom_call_target="tpu_custom_call" | custom-call | flops 268435456 | bytes 2097152 | tf_op jit(solution)/shard_map/own_tables/pallas_call | solution.py:331
  26.0 1.7 %collective-permute-done.1.source_table_ref = s32[24,256]{1,0:T(8,128)S(1)} collective-permute-done((s32[24,256]{1,0:T(8,128)S(1)}, s32[24,256]{1,0:T(8,128)S(1)}, u32[]{:S(2)}, u32[]{:S(2)}) %collective-permute-start.1) | collective-permute-done | bytes 24608 | tf_op jit(solution)/shard_map/ppermute | solution.py:329
  27.7 0.0 collective-permute-done.target_table_ref
  27.7 1.3 %all-to-all-done.x_ref = f32[16,64,128]{2,1,0:T(8,128)S(1)} async-done(((f32[16,64,128]{2,1,0:T(8,128)}), f32[16,64,128]{2,1,0:T(8,128)S(1)}, u32[]{:S(2)}, u32[]{:S(2)}) %all-to-all-start) | async-done | bytes 524320 | tf_op jit(solution)/shard_map/all_to_all | solution.py:328
  29.0 0.0 copy-start
  29.0 4.3 %two_sweeps.1 = f32[16,64,128]{2,1,0:T(8,128)S(1)} custom-call(s32[2]{0:T(128)S(1)} %pad_add_fusion.place_ref, f32[16,64,128]{2,1,0:T(8,128)S(1)} %all-to-all-done.x_ref, s32[24,256]{1,0:T(8,128)S(1)} %collective-permute-done.target_table_ref, s32[24,256]{1,0:T(8,128)S(1)} %collective-permute-done.1.source_table_ref, ...), custom_call_target="tpu_custom_call" | custom-call | flops 4294967296 | bytes 8388608 | tf_op jit(solution)/shard_map/two_sweeps/pallas_call | solution.py:353
  33.3 14.1 %all_to_all.10.parts_ref = f32[16,64,128]{2,1,0:T(8,128)S(1)} all-to-all(f32[16,64,128]{2,1,0:T(8,128)S(1)} %two_sweeps.1), channel_id=1, replica_groups={{0,1,2,3,4,5,6,7,8,9,10,11,12,13,14,15},{16,17,18,19,20,21,22,23,24,25,..., dimensions={0} | all-to-all | bytes 1048576 | tf_op jit(solution)/shard_map/all_to_all | solution.py:370
  47.4 0.0 copy-done
  47.4 1.2 %to_levels.1 = f32[128,512]{1,0:T(8,128)} custom-call(f32[16,64,128]{2,1,0:T(8,128)S(1)} %all_to_all.10.parts_ref, f32[128,128]{1,0:T(8,128)S(1)} %copy-done, bf16[512,512]{1,0:T(8,128)(2,1)S(1)} %get-tuple-element.22.back_ref), custom_call_target="tpu_custom_call" | custom-call | flops 83886080 | bytes 1048576 | tf_op jit(solution)/shard_map/to_levels/pallas_call | solution.py:371
Async XLA Ops:
  2.4 26.6 %all-to-all-start = ((f32[16,64,128]{2,1,0:T(8,128)}), f32[16,64,128]{2,1,0:T(8,128)S(1)}, u32[]{:S(2)}, u32[]{:S(2)}) async-start(f32[16,64,128]{2,1,0:T(8,128)} %get-tuple-element.14), calls=%async_computation | async-start | bytes 1048576 | tf_op jit(solution)/shard_map/all_to_all | solution.py:328
  19.8 7.9 %collective-permute-start.1 = (s32[24,256]{1,0:T(8,128)S(1)}, s32[24,256]{1,0:T(8,128)S(1)}, u32[]{:S(2)}, u32[]{:S(2)}) collective-permute-start(s32[24,256]{1,0:T(8,128)S(1)} %get-tuple-element.15.own_ref), channel_id=1, source_target_pairs={{0,504},{8,16},{16,8},{24,32},{32,24},{40,48},{48,40},{56,64},{64,... | collective-permute-start | bytes 73736 | tf_op jit(solution)/shard_map/ppermute | solution.py:329
  21.8 5.9 %collective-permute-start = (s32[24,256]{1,0:T(8,128)S(1)}, s32[24,256]{1,0:T(8,128)S(1)}, u32[]{:S(2)}, u32[]{:S(2)}) collective-permute-start(s32[24,256]{1,0:T(8,128)S(1)} %get-tuple-element.15.own_ref), channel_id=1, source_target_pairs={{0,8},{8,0},{16,24},{24,16},{32,40},{40,32},{48,56},{56,48},{64,72... | collective-permute-start | bytes 73736 | tf_op jit(solution)/shard_map/ppermute | solution.py:330
  29.0 18.4 %copy-start = (f32[128,128]{1,0:T(8,128)S(1)}, f32[128,128]{1,0:T(8,128)}, u32[]{:S(2)}) copy-start(f32[128,128]{1,0:T(8,128)} %levels_ref.1) | copy-start | bytes 196612

commit v6 on v5

--- a/solution.py
+++ b/solution.py
@@ -6,6 +6,18 @@
 from jax.experimental import pallas as pl
 from jax.experimental.pallas import tpu as pltpu
 from jax.sharding import PartitionSpec as P
+
+
+FIRST = 6
+
+
+def spot(block, device):
+    return 8 * block + (device - FIRST) % 8
+
+
+def half_spot(odd, half, quarter):
+    even_at, odd_at = (spot(at // 2, 4 * (at % 2) + quarter) for at in (half, 3 - half))
+    return jnp.where(odd, odd_at, even_at)
 
 
 def split(x):
@@ -91,7 +103,7 @@
         for quad in range(4):
             part = start[16 * group : 16 * group + 16, 128 * quad : 128 * quad + 128]
             for copy in range(2):
-                out_ref[8 * copy + group, 16 * quad : 16 * quad + 16, :] = part
+                out_ref[spot(copy, group), 16 * quad : 16 * quad + 16, :] = part
 
 
 def transpose_quads(parts):
@@ -213,9 +225,8 @@
         table_ref = source_table_ref if half == 2 else target_table_ref
         known[half] = write_picks(table_ref, half, odd, other_ref, OTHER[half])
     for half in range(4):
-        base = 4 * jnp.where(odd, 3 - half, half)
         for quad in range(4):
-            parts = [x_ref[base + j, 16 * quad : 16 * quad + 16, :] for j in range(4)]
+            parts = [x_ref[half_spot(odd, half, j), 16 * quad : 16 * quad + 16, :] for j in range(4)]
             for i, part in enumerate(transpose_quads(parts)):
                 rows = slice(64 * quad + 16 * i, 64 * quad + 16 * i + 16)
                 u_ref[half, rows, :] = part
@@ -253,7 +264,6 @@
                 s_ref[rows, 128 * place : 128 * place + 128] = value
     fixed = fix(high_ref, low_ref, s_ref[...])
     for place, half in enumerate((-2, -1, 0, 1)):
-        base = 4 * jnp.where(odd, 3 - place, place)
         for quad in range(4):
             parts = []
             for i in range(4):
@@ -265,7 +275,7 @@
                     value = value + u_ref[half, rows, :]
                 parts.append(value)
             for j, part in enumerate(transpose_quads(parts)):
-                out_ref[base + j, 16 * quad : 16 * quad + 16, :] = part
+                out_ref[half_spot(odd, place, j), 16 * quad : 16 * quad + 16, :] = part
 
 
 def to_levels_kernel(parts_ref, levels_ref, back_ref, out_ref, modes_ref):
@@ -273,7 +283,7 @@
         for quad in range(4):
             rows = slice(16 * quad, 16 * quad + 16)
             modes_ref[16 * group : 16 * group + 16, 128 * quad : 128 * quad + 128] = (
-                parts_ref[group, rows, :] + parts_ref[8 + group, rows, :]
+                parts_ref[spot(0, group), rows, :] + parts_ref[spot(1, group), rows, :]
             )
     high, low = split(dot3(levels_ref[...], modes_ref[...]))
     out_ref[...] = dot(high, back_ref[...]) + dot(low, back_ref[...])
@@ -300,10 +310,9 @@
 def body(blocks, levels_rhs, to_modes, from_modes, helmholtz, local_inverse, neighbor_ids, neighbor_count, orientation):
     axes = ("elem", "mode")
     parts = lax.axis_size("mode")
-    source_pairs = [
-        [((2 * k - 1 + i) % blocks) * parts + j for i in range(2) for j in range(parts)] for k in range(blocks // 2)
-    ]
-    target_pairs = [[(2 * k + i) * parts + j for i in range(2) for j in range(parts)] for k in range(blocks // 2)]
+    order = [(i, (j + FIRST) % parts) for i in range(2) for j in range(parts)]
+    source_pairs = [[((2 * k - 1 + i) % blocks) * parts + j for i, j in order] for k in range(blocks // 2)]
+    target_pairs = [[(2 * k + i) * parts + j for i, j in order] for k in range(blocks // 2)]
     source_swap = [(b, (((b + 1) ^ 1) - 1) % blocks) for b in range(blocks)]
     target_swap = [(b, b ^ 1) for b in range(blocks)]
     helmholtz = helmholtz[None]

time: 49 us -> 48.2 us (0.984)
  starting transfers between devices: 21.3 us -> 22.8 us
  waiting for transfers between devices: 2.95 us -> 1.56 us
  blocking collectives: 14.1 us -> 13.3 us
    all_to_all x1, starting transfers between devices: 17.4 us -> 18.7 us  [body(): lax.all_to_all(start, axes, 0, 0, axis_index_groups=source_pairs, tiled=T...]
    all_to_all x1, waiting for transfers between devices: 1.28 us -> 0.01 us  [body(): lax.all_to_all(start, axes, 0, 0, axis_index_groups=source_pairs, tiled=T...]
    all_to_all x1, blocking collectives: 14.1 us -> 13.3 us  [body(): lax.all_to_all(targets, axes, 0, 0, axis_index_groups=target_pairs, tiled...]
  transfers between devices with their start and end apart: 3 -> 3, of which waited for: 2 -> 1; matrix products, arithmetic and copies ran while one was open for 0% -> 0% of each run, Pallas kernels for 4% -> 5%
where the time goes in v6:
time: 48.2 us; the launch traced here: 47.8 us
  starting transfers between devices  22.8 us (47%)
  blocking collectives  13.3 us (28%)
  Pallas kernels  10.1 us (21%)
  waiting for transfers between devices  1.56 us (3%)
    all_to_all x1, starting transfers between devices, body(): lax.all_to_all(start, axes, 0, 0, axis_index_groups=source_pairs, tiled=T...  18.7 us
    all_to_all x1, blocking collectives, body(): lax.all_to_all(targets, axes, 0, 0, axis_index_groups=target_pairs, tiled...  13.3 us
    pallas_call x1, Pallas kernels, body(): pl.pallas_call(sweep_kernel, out_shape=pltpu.VMEM((16, 64, 128), jnp.floa...  4.37 us
    pallas_call x1, Pallas kernels, body(): pl.pallas_call(to_modes_kernel, out_shape=(pltpu.VMEM((16, 64, 128), jnp....  2.38 us
    pallas_call x1, Pallas kernels, body(): pl.pallas_call(tables_kernel, out_shape=(pltpu.VMEM((4, 6, 128, 256), jnp...  2.17 us
    ppermute x1, starting transfers between devices, body(): source_table = lax.ppermute(own, 'elem', source_swap)  2.13 us
    ppermute x1, starting transfers between devices, body(): target_table = lax.ppermute(own, 'elem', target_swap)  1.92 us
    ppermute x1, waiting for transfers between devices, body(): source_table = lax.ppermute(own, 'elem', source_swap)  1.56 us
  transfers between devices with their start and end apart: 3, of which 1 were waited for; matrix products, arithmetic and copies ran while one was open for 0% of the time, Pallas kernels for 5%

profile of v6, /device:TPU:1, one launch (start us, length us, event | category | flops | bytes accessed | tf_op | source)
XLA Modules:
  0.0 47.8 jit_solution(459813739891214363)
XLA Ops:
  0.0 2.4 %to_modes_chunks.1 = (f32[16,64,128]{2,1,0:T(8,128)}, s32[24,256]{1,0:T(8,128)S(1)}) custom-call(f32[128,512]{1,0:T(8,128)} %rhs_hbm.1, f32[128,128]{1,0:T(8,128)} %modes_hbm.1, f32[1,128]{1,0:T(1,128)} %bitcast.5, s32[8,256]{1,0:T(8,128)} %ids_hbm.1, s32[8,256]{1,0:T(8,128)} %orientation_hbm.1, s32[1,256]{1,0:T(1,128)} %bitcast.4), custom_call_target="tpu_custom_call" | custom-call | flops 83886080 | bytes 1048576 | tf_op jit(solution)/shard_map/to_modes_chunks/pallas_call | solution.py:321
  2.4 18.7 %all-to-all-start = ((f32[16,64,128]{2,1,0:T(8,128)}), f32[16,64,128]{2,1,0:T(8,128)S(1)}, u32[]{:S(2)}, u32[]{:S(2)}) async-start(f32[16,64,128]{2,1,0:T(8,128)} %get-tuple-element.14), calls=%async_computation | async-start | bytes 1048576 | tf_op jit(solution)/shard_map/all_to_all | solution.py:337
  21.1 2.1 %collective-permute-start.1 = (s32[24,256]{1,0:T(8,128)S(1)}, s32[24,256]{1,0:T(8,128)S(1)}, u32[]{:S(2)}, u32[]{:S(2)}) collective-permute-start(s32[24,256]{1,0:T(8,128)S(1)} %get-tuple-element.15.own_ref), channel_id=1, source_target_pairs={{0,504},{8,16},{16,8},{24,32},{32,24},{40,48},{48,40},{56,64},{64,... | collective-permute-start | bytes 73736 | tf_op jit(solution)/shard_map/ppermute | solution.py:338
  23.2 1.9 %collective-permute-start = (s32[24,256]{1,0:T(8,128)S(1)}, s32[24,256]{1,0:T(8,128)S(1)}, u32[]{:S(2)}, u32[]{:S(2)}) collective-permute-start(s32[24,256]{1,0:T(8,128)S(1)} %get-tuple-element.15.own_ref), channel_id=1, source_target_pairs={{0,8},{8,0},{16,24},{24,16},{32,40},{40,32},{48,56},{56,48},{64,72... | collective-permute-start | bytes 73736 | tf_op jit(solution)/shard_map/ppermute | solution.py:339
  25.2 0.1 pad_add_fusion.place_ref
  25.3 2.2 %own_tables.1 = (bf16[4,6,128,256]{3,2,1,0:T(8,128)(2,1)S(1)}, s32[2,8,128]{2,1,0:T(8,128)S(1)}, f32[16,128]{1,0:T(8,128)S(1)}, f32[2,8,128]{2,1,0:T(8,128)S(1)}...) custom-call(s32[2]{0:T(128)S(1)} %pad_add_fusion.place_ref, ...), custom_call_target="tpu_custom_call" | custom-call | flops 268435456 | bytes 2097152 | tf_op jit(solution)/shard_map/own_tables/pallas_call | solution.py:340
  27.4 1.6 %collective-permute-done.1.source_table_ref = s32[24,256]{1,0:T(8,128)S(1)} collective-permute-done((s32[24,256]{1,0:T(8,128)S(1)}, s32[24,256]{1,0:T(8,128)S(1)}, u32[]{:S(2)}, u32[]{:S(2)}) %collective-permute-start.1) | collective-permute-done | bytes 24608 | tf_op jit(solution)/shard_map/ppermute | solution.py:338
  29.0 0.0 collective-permute-done.target_table_ref
  29.0 0.0 all-to-all-done.x_ref
  29.0 0.0 copy-start
  29.0 4.4 %two_sweeps.1 = f32[16,64,128]{2,1,0:T(8,128)S(1)} custom-call(s32[2]{0:T(128)S(1)} %pad_add_fusion.place_ref, f32[16,64,128]{2,1,0:T(8,128)S(1)} %all-to-all-done.x_ref, s32[24,256]{1,0:T(8,128)S(1)} %collective-permute-done.target_table_ref, s32[24,256]{1,0:T(8,128)S(1)} %collective-permute-done.1.source_table_ref, ...), custom_call_target="tpu_custom_call" | custom-call | flops 4294967296 | bytes 8388608 | tf_op jit(solution)/shard_map/two_sweeps/pallas_call | solution.py:362
  33.4 13.3 %all_to_all.10.parts_ref = f32[16,64,128]{2,1,0:T(8,128)S(1)} all-to-all(f32[16,64,128]{2,1,0:T(8,128)S(1)} %two_sweeps.1), channel_id=1, replica_groups={{6,7,0,1,2,3,4,5,14,15,8,9,10,11,12,13},{22,23,16,17,18,19,20,21,30,31,..., dimensions={0} | all-to-all | bytes 1048576 | tf_op jit(solution)/shard_map/all_to_all | solution.py:379
  46.6 0.0 copy-done
  46.6 1.2 %to_levels.1 = f32[128,512]{1,0:T(8,128)} custom-call(f32[16,64,128]{2,1,0:T(8,128)S(1)} %all_to_all.10.parts_ref, f32[128,128]{1,0:T(8,128)S(1)} %copy-done, bf16[512,512]{1,0:T(8,128)(2,1)S(1)} %get-tuple-element.22.back_ref), custom_call_target="tpu_custom_call" | custom-call | flops 83886080 | bytes 1048576 | tf_op jit(solution)/shard_map/to_levels/pallas_call | solution.py:380
Async XLA Ops:
  2.4 26.6 %all-to-all-start = ((f32[16,64,128]{2,1,0:T(8,128)}), f32[16,64,128]{2,1,0:T(8,128)S(1)}, u32[]{:S(2)}, u32[]{:S(2)}) async-start(f32[16,64,128]{2,1,0:T(8,128)} %get-tuple-element.14), calls=%async_computation | async-start | bytes 1048576 | tf_op jit(solution)/shard_map/all_to_all | solution.py:337
  21.1 7.9 %collective-permute-start.1 = (s32[24,256]{1,0:T(8,128)S(1)}, s32[24,256]{1,0:T(8,128)S(1)}, u32[]{:S(2)}, u32[]{:S(2)}) collective-permute-start(s32[24,256]{1,0:T(8,128)S(1)} %get-tuple-element.15.own_ref), channel_id=1, source_target_pairs={{0,504},{8,16},{16,8},{24,32},{32,24},{40,48},{48,40},{56,64},{64,... | collective-permute-start | bytes 73736 | tf_op jit(solution)/shard_map/ppermute | solution.py:338
  23.2 5.7 %collective-permute-start = (s32[24,256]{1,0:T(8,128)S(1)}, s32[24,256]{1,0:T(8,128)S(1)}, u32[]{:S(2)}, u32[]{:S(2)}) collective-permute-start(s32[24,256]{1,0:T(8,128)S(1)} %get-tuple-element.15.own_ref), channel_id=1, source_target_pairs={{0,8},{8,0},{16,24},{24,16},{32,40},{40,32},{48,56},{56,48},{64,72... | collective-permute-start | bytes 73736 | tf_op jit(solution)/shard_map/ppermute | solution.py:339
  29.0 17.6 %copy-start = (f32[128,128]{1,0:T(8,128)S(1)}, f32[128,128]{1,0:T(8,128)}, u32[]{:S(2)}) copy-start(f32[128,128]{1,0:T(8,128)} %levels_ref.1) | copy-start | bytes 196612

commit v7 on v5

--- a/solution.py
+++ b/solution.py
@@ -6,6 +6,18 @@
 from jax.experimental import pallas as pl
 from jax.experimental.pallas import tpu as pltpu
 from jax.sharding import PartitionSpec as P
+
+
+FIRST, SECOND = 6, 2
+
+
+def spot(block, device, start):
+    return 8 * block + (device - start) % 8
+
+
+def half_spot(odd, half, quarter, start):
+    even_at, odd_at = (spot(at // 2, 4 * (at % 2) + quarter, start) for at in (half, 3 - half))
+    return jnp.where(odd, odd_at, even_at)
 
 
 def split(x):
@@ -91,7 +103,7 @@
         for quad in range(4):
             part = start[16 * group : 16 * group + 16, 128 * quad : 128 * quad + 128]
             for copy in range(2):
-                out_ref[8 * copy + group, 16 * quad : 16 * quad + 16, :] = part
+                out_ref[spot(copy, group, FIRST), 16 * quad : 16 * quad + 16, :] = part
 
 
 def transpose_quads(parts):
@@ -213,9 +225,8 @@
         table_ref = source_table_ref if half == 2 else target_table_ref
         known[half] = write_picks(table_ref, half, odd, other_ref, OTHER[half])
     for half in range(4):
-        base = 4 * jnp.where(odd, 3 - half, half)
         for quad in range(4):
-            parts = [x_ref[base + j, 16 * quad : 16 * quad + 16, :] for j in range(4)]
+            parts = [x_ref[half_spot(odd, half, j, FIRST), 16 * quad : 16 * quad + 16, :] for j in range(4)]
             for i, part in enumerate(transpose_quads(parts)):
                 rows = slice(64 * quad + 16 * i, 64 * quad + 16 * i + 16)
                 u_ref[half, rows, :] = part
@@ -253,7 +264,6 @@
                 s_ref[rows, 128 * place : 128 * place + 128] = value
     fixed = fix(high_ref, low_ref, s_ref[...])
     for place, half in enumerate((-2, -1, 0, 1)):
-        base = 4 * jnp.where(odd, 3 - place, place)
         for quad in range(4):
             parts = []
             for i in range(4):
@@ -265,7 +275,7 @@
                     value = value + u_ref[half, rows, :]
                 parts.append(value)
             for j, part in enumerate(transpose_quads(parts)):
-                out_ref[base + j, 16 * quad : 16 * quad + 16, :] = part
+                out_ref[half_spot(odd, place, j, SECOND), 16 * quad : 16 * quad + 16, :] = part
 
 
 def to_levels_kernel(parts_ref, levels_ref, back_ref, out_ref, modes_ref):
@@ -273,7 +283,7 @@
         for quad in range(4):
             rows = slice(16 * quad, 16 * quad + 16)
             modes_ref[16 * group : 16 * group + 16, 128 * quad : 128 * quad + 128] = (
-                parts_ref[group, rows, :] + parts_ref[8 + group, rows, :]
+                parts_ref[spot(0, group, SECOND), rows, :] + parts_ref[spot(1, group, SECOND), rows, :]
             )
     high, low = split(dot3(levels_ref[...], modes_ref[...]))
     out_ref[...] = dot(high, back_ref[...]) + dot(low, back_ref[...])
@@ -300,10 +310,9 @@
 def body(blocks, levels_rhs, to_modes, from_modes, helmholtz, local_inverse, neighbor_ids, neighbor_count, orientation):
     axes = ("elem", "mode")
     parts = lax.axis_size("mode")
-    source_pairs = [
-        [((2 * k - 1 + i) % blocks) * parts + j for i in range(2) for j in range(parts)] for k in range(blocks // 2)
-    ]
-    target_pairs = [[(2 * k + i) * parts + j for i in range(2) for j in range(parts)] for k in range(blocks // 2)]
+    order = lambda start: [(i, (j + start) % parts) for i in range(2) for j in range(parts)]
+    source_pairs = [[((2 * k - 1 + i) % blocks) * parts + j for i, j in order(FIRST)] for k in range(blocks // 2)]
+    target_pairs = [[(2 * k + i) * parts + j for i, j in order(SECOND)] for k in range(blocks // 2)]
     source_swap = [(b, (((b + 1) ^ 1) - 1) % blocks) for b in range(blocks)]
     target_swap = [(b, b ^ 1) for b in range(blocks)]
     helmholtz = helmholtz[None]

time: 49 us -> 49.5 us (1.010)
  starting transfers between devices: 21.3 us -> 22.8 us
  waiting for transfers between devices: 2.95 us -> 1.56 us
  blocking collectives: 14.1 us -> 14.6 us
    all_to_all x1, starting transfers between devices: 17.4 us -> 18.7 us  [body(): lax.all_to_all(start, axes, 0, 0, axis_index_groups=source_pairs, tiled=T...]
    all_to_all x1, waiting for transfers between devices: 1.28 us -> 0.01 us  [body(): lax.all_to_all(start, axes, 0, 0, axis_index_groups=source_pairs, tiled=T...]
    all_to_all x1, blocking collectives: 14.1 us -> 14.6 us  [body(): lax.all_to_all(targets, axes, 0, 0, axis_index_groups=target_pairs, tiled...]
  transfers between devices with their start and end apart: 3 -> 3, of which waited for: 2 -> 1; matrix products, arithmetic and copies ran while one was open for 0% -> 0% of each run, Pallas kernels for 4% -> 4%
where the time goes in v7:
time: 49.5 us; the launch traced here: 49.2 us
  starting transfers between devices  22.8 us (46%)
  blocking collectives  14.6 us (29%)
  Pallas kernels  10.1 us (20%)
  waiting for transfers between devices  1.56 us (3%)
    all_to_all x1, starting transfers between devices, body(): lax.all_to_all(start, axes, 0, 0, axis_index_groups=source_pairs, tiled=T...  18.7 us
    all_to_all x1, blocking collectives, body(): lax.all_to_all(targets, axes, 0, 0, axis_index_groups=target_pairs, tiled...  14.6 us
    pallas_call x1, Pallas kernels, body(): pl.pallas_call(sweep_kernel, out_shape=pltpu.VMEM((16, 64, 128), jnp.floa...  4.34 us
    pallas_call x1, Pallas kernels, body(): pl.pallas_call(to_modes_kernel, out_shape=(pltpu.VMEM((16, 64, 128), jnp....  2.38 us
    pallas_call x1, Pallas kernels, body(): pl.pallas_call(tables_kernel, out_shape=(pltpu.VMEM((4, 6, 128, 256), jnp...  2.17 us
    ppermute x1, starting transfers between devices, body(): source_table = lax.ppermute(own, 'elem', source_swap)  2.13 us
    ppermute x1, starting transfers between devices, body(): target_table = lax.ppermute(own, 'elem', target_swap)  1.92 us
    ppermute x1, waiting for transfers between devices, body(): source_table = lax.ppermute(own, 'elem', source_swap)  1.56 us
  transfers between devices with their start and end apart: 3, of which 1 were waited for; matrix products, arithmetic and copies ran while one was open for 0% of the time, Pallas kernels for 4%

profile of v7, /device:TPU:1, one launch (start us, length us, event | category | flops | bytes accessed | tf_op | source)
XLA Modules:
  0.0 49.2 jit_solution(10286915003918056570)
XLA Ops:
  0.0 2.4 %to_modes_chunks.1 = (f32[16,64,128]{2,1,0:T(8,128)}, s32[24,256]{1,0:T(8,128)S(1)}) custom-call(f32[128,512]{1,0:T(8,128)} %rhs_hbm.1, f32[128,128]{1,0:T(8,128)} %modes_hbm.1, f32[1,128]{1,0:T(1,128)} %bitcast.5, s32[8,256]{1,0:T(8,128)} %ids_hbm.1, s32[8,256]{1,0:T(8,128)} %orientation_hbm.1, s32[1,256]{1,0:T(1,128)} %bitcast.4), custom_call_target="tpu_custom_call" | custom-call | flops 83886080 | bytes 1048576 | tf_op jit(solution)/shard_map/to_modes_chunks/pallas_call | solution.py:321
  2.4 18.7 %all-to-all-start = ((f32[16,64,128]{2,1,0:T(8,128)}), f32[16,64,128]{2,1,0:T(8,128)S(1)}, u32[]{:S(2)}, u32[]{:S(2)}) async-start(f32[16,64,128]{2,1,0:T(8,128)} %get-tuple-element.14), calls=%async_computation | async-start | bytes 1048576 | tf_op jit(solution)/shard_map/all_to_all | solution.py:337
  21.1 2.1 %collective-permute-start.1 = (s32[24,256]{1,0:T(8,128)S(1)}, s32[24,256]{1,0:T(8,128)S(1)}, u32[]{:S(2)}, u32[]{:S(2)}) collective-permute-start(s32[24,256]{1,0:T(8,128)S(1)} %get-tuple-element.15.own_ref), channel_id=1, source_target_pairs={{0,504},{8,16},{16,8},{24,32},{32,24},{40,48},{48,40},{56,64},{64,... | collective-permute-start | bytes 73736 | tf_op jit(solution)/shard_map/ppermute | solution.py:338
  23.2 1.9 %collective-permute-start = (s32[24,256]{1,0:T(8,128)S(1)}, s32[24,256]{1,0:T(8,128)S(1)}, u32[]{:S(2)}, u32[]{:S(2)}) collective-permute-start(s32[24,256]{1,0:T(8,128)S(1)} %get-tuple-element.15.own_ref), channel_id=1, source_target_pairs={{0,8},{8,0},{16,24},{24,16},{32,40},{40,32},{48,56},{56,48},{64,72... | collective-permute-start | bytes 73736 | tf_op jit(solution)/shard_map/ppermute | solution.py:339
  25.2 0.1 pad_add_fusion.place_ref
  25.3 2.2 %own_tables.1 = (bf16[4,6,128,256]{3,2,1,0:T(8,128)(2,1)S(1)}, s32[2,8,128]{2,1,0:T(8,128)S(1)}, f32[16,128]{1,0:T(8,128)S(1)}, f32[2,8,128]{2,1,0:T(8,128)S(1)}...) custom-call(s32[2]{0:T(128)S(1)} %pad_add_fusion.place_ref, ...), custom_call_target="tpu_custom_call" | custom-call | flops 268435456 | bytes 2097152 | tf_op jit(solution)/shard_map/own_tables/pallas_call | solution.py:340
  27.4 1.6 %collective-permute-done.1.source_table_ref = s32[24,256]{1,0:T(8,128)S(1)} collective-permute-done((s32[24,256]{1,0:T(8,128)S(1)}, s32[24,256]{1,0:T(8,128)S(1)}, u32[]{:S(2)}, u32[]{:S(2)}) %collective-permute-start.1) | collective-permute-done | bytes 24608 | tf_op jit(solution)/shard_map/ppermute | solution.py:338
  29.0 0.0 collective-permute-done.target_table_ref
  29.0 0.0 all-to-all-done.x_ref
  29.0 0.0 copy-start
  29.0 4.3 %two_sweeps.1 = f32[16,64,128]{2,1,0:T(8,128)S(1)} custom-call(s32[2]{0:T(128)S(1)} %pad_add_fusion.place_ref, f32[16,64,128]{2,1,0:T(8,128)S(1)} %all-to-all-done.x_ref, s32[24,256]{1,0:T(8,128)S(1)} %collective-permute-done.target_table_ref, s32[24,256]{1,0:T(8,128)S(1)} %collective-permute-done.1.source_table_ref, ...), custom_call_target="tpu_custom_call" | custom-call | flops 4294967296 | bytes 8388608 | tf_op jit(solution)/shard_map/two_sweeps/pallas_call | solution.py:362
  33.3 14.6 %all_to_all.10.parts_ref = f32[16,64,128]{2,1,0:T(8,128)S(1)} all-to-all(f32[16,64,128]{2,1,0:T(8,128)S(1)} %two_sweeps.1), channel_id=1, replica_groups={{2,3,4,5,6,7,0,1,10,11,12,13,14,15,8,9},{18,19,20,21,22,23,16,17,26,27,..., dimensions={0} | all-to-all | bytes 1048576 | tf_op jit(solution)/shard_map/all_to_all | solution.py:379
  47.9 0.0 copy-done
  47.9 1.2 %to_levels.1 = f32[128,512]{1,0:T(8,128)} custom-call(f32[16,64,128]{2,1,0:T(8,128)S(1)} %all_to_all.10.parts_ref, f32[128,128]{1,0:T(8,128)S(1)} %copy-done, bf16[512,512]{1,0:T(8,128)(2,1)S(1)} %get-tuple-element.22.back_ref), custom_call_target="tpu_custom_call" | custom-call | flops 83886080 | bytes 1048576 | tf_op jit(solution)/shard_map/to_levels/pallas_call | solution.py:380
Async XLA Ops:
  2.4 26.6 %all-to-all-start = ((f32[16,64,128]{2,1,0:T(8,128)}), f32[16,64,128]{2,1,0:T(8,128)S(1)}, u32[]{:S(2)}, u32[]{:S(2)}) async-start(f32[16,64,128]{2,1,0:T(8,128)} %get-tuple-element.14), calls=%async_computation | async-start | bytes 1048576 | tf_op jit(solution)/shard_map/all_to_all | solution.py:337
  21.1 7.9 %collective-permute-start.1 = (s32[24,256]{1,0:T(8,128)S(1)}, s32[24,256]{1,0:T(8,128)S(1)}, u32[]{:S(2)}, u32[]{:S(2)}) collective-permute-start(s32[24,256]{1,0:T(8,128)S(1)} %get-tuple-element.15.own_ref), channel_id=1, source_target_pairs={{0,504},{8,16},{16,8},{24,32},{32,24},{40,48},{48,40},{56,64},{64,... | collective-permute-start | bytes 73736 | tf_op jit(solution)/shard_map/ppermute | solution.py:338
  23.2 5.7 %collective-permute-start = (s32[24,256]{1,0:T(8,128)S(1)}, s32[24,256]{1,0:T(8,128)S(1)}, u32[]{:S(2)}, u32[]{:S(2)}) collective-permute-start(s32[24,256]{1,0:T(8,128)S(1)} %get-tuple-element.15.own_ref), channel_id=1, source_target_pairs={{0,8},{8,0},{16,24},{24,16},{32,40},{40,32},{48,56},{56,48},{64,72... | collective-permute-start | bytes 73736 | tf_op jit(solution)/shard_map/ppermute | solution.py:339
  29.0 19.0 %copy-start = (f32[128,128]{1,0:T(8,128)S(1)}, f32[128,128]{1,0:T(8,128)}, u32[]{:S(2)}) copy-start(f32[128,128]{1,0:T(8,128)} %levels_ref.1) | copy-start | bytes 196612
